TPU v7x, 128 devices: a whole 4x4x4 slice. The times are simulated.
128 devices in a mesh: ctx: 16 (over z, x_lo, core), tp: 8 (over x_hi, y).
Axes of the slice: x: 4 (x_hi: 2, x_lo: 2; x = x_hi * 2 + x_lo), y: 4, z: 4, core: 2. Of those that a mesh axis runs over, the one named last changes fastest.
Arguments:
- hidden_in: bfloat16 [16384, 5376], P(('ctx', 'tp')), may hold values from -6 to 6
- in_gain: float32 [5376], replicated, may hold values from 0.1 to 1.9
- query_weight: bfloat16 [5376, 4096], P('ctx', 'tp'), may hold values from -0.078125 to 0.078125
- key_weight: bfloat16 [5376, 2048], P('ctx', 'tp'), may hold values from -0.078125 to 0.078125
- value_weight: bfloat16 [5376, 2048], P('ctx', 'tp'), may hold values from -0.078125 to 0.078125
- out_weight: bfloat16 [4096, 5376], P('tp', 'ctx'), may hold values from -0.09375 to 0.09375
- q_gain: float32 [128], replicated, may hold values from 0.5 to 16
- k_gain: float32 [128], replicated, may hold values from 0.5 to 16
- post_gain: float32 [5376], replicated, may hold values from 0.1 to 1.9
Outputs:
- layer_out: bfloat16 [16384, 5376], P(('ctx', 'tp'))
All inputs are finite; a program needn't handle non-finite values.
Results may differ from a plain program's by a relative error of at most 0.015.
The roundings to bfloat16 on the way count: a program that leaves them out, or rounds other values in their place, can miss the bound.
Values may be sent and summed in bfloat16 or wider, within the bound.
A program may use at most 192 MiB of HBM per device.

v0:
```python
import jax
import jax.numpy as jnp
from jax import lax
from jax.sharding import PartitionSpec as P

WINDOW = 1024
SCALAR = 168


def from_behind(array, axis, by):
    peers = lax.axis_size(axis)
    pairs = [(i, i + by) for i in range(peers) if 0 <= i + by < peers]
    return lax.ppermute(array, axis, pairs)


def rms_scale(values, gain):
    return values * lax.rsqrt(jnp.mean(values * values, axis=-1, keepdims=True) + 1e-06) * gain


def rotate(vectors, positions):
    half_dim = vectors.shape[-1] // 2
    frequency = 10000.0 ** (-(jnp.arange(half_dim, dtype=jnp.float32) * 2.0 / vectors.shape[-1]))
    angles = positions.astype(jnp.float32)[:, None] * frequency[None, :]
    cosine = jnp.cos(angles)[:, None, :]
    sine_part = jnp.sin(angles)[:, None, :]
    first_half = vectors[..., :half_dim]
    second_half = vectors[..., half_dim:]
    return jnp.concatenate(
        [
            first_half * cosine - second_half * sine_part,
            second_half * cosine + first_half * sine_part,
        ],
        axis=-1,
    )


def attend(queries, keys, values, query_pos, key_pos):
    row_count, query_heads, head_dim = queries.shape
    key_heads = keys.shape[1]
    group_size = query_heads // key_heads
    grouped = queries.reshape(row_count, key_heads, group_size, head_dim)
    scores = jnp.einsum("rhgd,khd->hgrk", grouped, keys, preferred_element_type=jnp.float32)
    offset = query_pos[:, None] - key_pos[None, :]
    allowed = (offset >= 0) & (offset < WINDOW) & (key_pos[None, :] >= 0)
    scores = jnp.where(allowed, scores * float(SCALAR) ** (-0.5), -1e30)
    row_max = jnp.max(scores, axis=-1, keepdims=True)
    expo = jnp.where(allowed, jnp.exp(scores - row_max), 0.0)
    weights = (expo / jnp.sum(expo, axis=-1, keepdims=True)).astype(jnp.bfloat16)
    mixed = jnp.einsum("hgrk,khd->rhgd", weights, values, preferred_element_type=jnp.float32)
    return mixed.astype(jnp.bfloat16).reshape(row_count, query_heads * head_dim)


def attend_blocks(queries, keys, values, query_pos, key_pos):
    row_count = queries.shape[0]
    piece_rows = min(row_count, 512)
    outputs = []
    for first in range(0, row_count, piece_rows):
        outputs.append(
            attend(
                queries[first : first + piece_rows],
                keys[first : first + piece_rows + WINDOW],
                values[first : first + piece_rows + WINDOW],
                query_pos[first : first + piece_rows],
                key_pos[first : first + piece_rows + WINDOW],
            )
        )
    return jnp.concatenate(outputs, axis=0)


def add_product(left, weight_piece):
    return jnp.dot(left, weight_piece, preferred_element_type=jnp.float32)


def reach_keys(keys, values):
    got_keys, got_values = from_behind((keys, values), "ctx", 1)
    far_keys = [got_keys]
    far_values = [got_values]
    return (
        jnp.concatenate(far_keys + [keys], axis=0),
        jnp.concatenate(far_values + [values], axis=0),
    )


def per_device(
    hidden_in,
    in_gain,
    query_weight,
    key_weight,
    value_weight,
    out_weight,
    q_gain,
    k_gain,
    post_gain,
):
    normed = rms_scale(hidden_in.astype(jnp.float32), in_gain).astype(jnp.bfloat16)
    block = lax.all_gather(normed, "tp", axis=0, tiled=True)
    block_rows = block.shape[0]
    head_dim = q_gain.shape[0]
    block_start = lax.axis_index("ctx") * block_rows
    own_pos = block_start + jnp.arange(block_rows, dtype=jnp.int32)
    wide_pos = block_start - WINDOW + jnp.arange(WINDOW + block_rows, dtype=jnp.int32)
    kv_rows = block.shape[0]
    query_raw = add_product(block, lax.all_gather(query_weight, "ctx", axis=0, tiled=True))
    key_raw = add_product(block, lax.all_gather(key_weight, "ctx", axis=0, tiled=True))
    value_raw = add_product(block, lax.all_gather(value_weight, "ctx", axis=0, tiled=True))
    queries = rotate(
        rms_scale(query_raw.reshape(block_rows, -1, head_dim), q_gain), own_pos
    ).astype(jnp.bfloat16)
    keys = rotate(rms_scale(key_raw.reshape(kv_rows, -1, head_dim), k_gain), own_pos).astype(
        jnp.bfloat16
    )
    values = value_raw.astype(jnp.bfloat16).reshape(kv_rows, -1, head_dim)
    keys, values = reach_keys(keys, values)
    attended = attend_blocks(queries, keys, values, own_pos, wide_pos)
    out_full = lax.all_gather(out_weight, "ctx", axis=1, tiled=True)
    projected = lax.psum_scatter(
        jnp.dot(attended, out_full, preferred_element_type=jnp.float32).astype(jnp.bfloat16),
        "tp",
        scatter_dimension=0,
        tiled=True,
    ).astype(jnp.float32)
    return (hidden_in.astype(jnp.float32) + rms_scale(projected, post_gain)).astype(jnp.bfloat16)


def solution(mesh):
    in_specs = (
        P(("ctx", "tp"), None),
        P(),
        P("ctx", "tp"),
        P("ctx", "tp"),
        P("ctx", "tp"),
        P("tp", "ctx"),
        P(),
        P(),
        P(),
    )
    out_specs = P(("ctx", "tp"), None)
    return jax.shard_map(
        per_device, mesh=mesh, in_specs=in_specs, out_specs=out_specs, check_vma=False
    )
```

profile of v0, /device:TPU:0, one launch (start us, length us, event | category | flops | bytes accessed | tf_op | source)
XLA Modules:
  0.0 467.0 jit_solution(9747930731905477069)
XLA Ops:
  6.5 0.7 all-gather.10.cloned.1.call-update
  7.3 0.0 all-gather.6.cloned.1.call-start
  7.3 1.7 fusion.18
  9.0 2.8 fusion.20
  11.8 0.0 all-gather.6.cloned.1.call-update
  11.8 0.0 all-gather.8.cloned.1.call-start
  11.9 0.7 all-gather.8.cloned.1.call-update
  12.6 0.0 all-gather.12.cloned.1.call-start
  12.6 0.5 all-gather.12.cloned.1.call-update
  13.1 0.0 all-gather.14.cloned.1.call-start
  13.2 0.5 all-gather.14.cloned.1.call-update
  13.7 0.0 reduce-scatter.2.cloned.1.call-start
  13.9 1.0 multiply_cosine_fusion
  14.9 0.2 copy.18
  15.1 0.2 copy.19
  15.3 1.2 fusion.13
  16.5 2.0 fusion.15
  18.5 28.1 %all-gather.10.cloned.1.call-done = bf16[5376,256]{1,0:T(8,128)(2,1)} async-done(((bf16[336,256]{1,0:T(8,128)(2,1)}), bf16[5376,256]{1,0:T(8,128)(2,1)}) %all-gather.10.cloned.1.call-update) | async-done | bytes 2752528 | tf_op jit(solution)/shard_map/all_gather | solution.py:104
  46.5 132.4 %all-gather.6.cloned.1.call-done = bf16[1024,5376]{1,0:T(8,128)(2,1)} async-done(((bf16[128,5376]{1,0:T(8,128)(2,1)}), bf16[1024,5376]{1,0:T(8,128)(2,1)}) %all-gather.6.cloned.1.call-update) | async-done | bytes 11010064 | tf_op jit(solution)/shard_map/all_gather | solution.py:96
  178.9 9.0 %multiply_reduce_fusion.1 = (f32[1024,2]{0,1:T(2,128)S(1)}, f32[1024,256]{0,1:T(8,128)}) fusion(bf16[1024,5376]{1,0:T(8,128)(2,1)} %all-gather.6.cloned.1.call-done, bf16[5376,256]{1,0:T(8,128)(2,1)} %all-gather.10.cloned.1.call-done), kind=kOutput, calls=%fused_computation.58 | convolution fusion | flops 2819094528 | bytes 14819328 | tf_op jit(solution)/shard_map/dot_general | solution.py:71
  187.9 1.5 copy.17
  189.5 0.3 multiply_multiply_fusion.1
  189.8 0.5 subtract_convert_fusion.1
  190.3 1.1 pad_maximum_fusion.2
  191.4 1.3 collective-permute-start.1
  192.7 24.8 %all-gather.8.cloned.1.call-done = bf16[5376,256]{1,0:T(8,128)(2,1)} async-done(((bf16[336,256]{1,0:T(8,128)(2,1)}), bf16[5376,256]{1,0:T(8,128)(2,1)}) %all-gather.8.cloned.1.call-update) | async-done | bytes 2752528 | tf_op jit(solution)/shard_map/all_gather | solution.py:105
  217.6 8.8 %convolution_convert_fusion.1 = bf16[1024,256]{0,1:T(8,128)(2,1)} fusion(bf16[1024,5376]{1,0:T(8,128)(2,1)} %all-gather.6.cloned.1.call-done, bf16[5376,256]{1,0:T(8,128)(2,1)} %all-gather.8.cloned.1.call-done), kind=kOutput, calls=%fused_computation.44 | convolution fusion | flops 2818834432 | bytes 14286848 | tf_op jit(solution)/shard_map/dot_general | solution.py:71
  226.3 3.1 collective-permute-start
  229.4 35.3 %all-gather.12.cloned.1.call-done = bf16[5376,512]{1,0:T(8,128)(2,1)} async-done(((bf16[336,512]{1,0:T(8,128)(2,1)}), bf16[5376,512]{1,0:T(8,128)(2,1)}) %all-gather.12.cloned.1.call-update) | async-done | bytes 5505040 | tf_op jit(solution)/shard_map/all_gather | solution.py:103
  264.7 10.3 %multiply_reduce_fusion = (f32[1024,4]{0,1:T(4,128)S(1)}, f32[1024,512]{0,1:T(8,128)S(1)}) fusion(bf16[1024,5376]{1,0:T(8,128)(2,1)} %all-gather.6.cloned.1.call-done, bf16[5376,512]{1,0:T(8,128)(2,1)} %all-gather.12.cloned.1.call-done), kind=kOutput, calls=%fused_computation.39 | convolution fusion | flops 5638189056 | bytes 18628608 | tf_op jit(solution)/shard_map/dot_general | solution.py:71
  275.1 0.5 multiply_multiply_fusion
  275.6 0.4 subtract_convert_fusion
  275.9 1.1 fusion.39
  277.0 0.0 collective-permute-done.1
  277.0 0.3 maximum_maximum_fusion
  277.3 9.5 %fusion.51 = (f32[2,2,512]{2,1,0:T(2,128)S(1)}, f32[2,2,512,1536]{2,3,1,0:T(8,128)}) fusion(pred[512,1536]{0,1:T(8,128)(4,1)S(1)} %fusion.13, bf16[512,2,2,128]{0,3,2,1:T(8,128)(2,1)} %bitcast.89, bf16[2048,2,128]{2,0,1:T(8,128)(2,1)S(1)} %maximum_maximum_fusion), kind=kOutput, calls=%fused_computation.93 | convolution fusion | flops 821036544 | bytes 15474688 | tf_op jit(solution)/shard_map/sub | solution.py:47
  286.8 0.0 copy-done.1
  286.8 8.3 %fusion.50 = (f32[2,2,512]{2,1,0:T(2,128)S(1)}, f32[2,2,512,1536]{2,3,1,0:T(8,128)}) fusion(pred[512,1536]{0,1:T(8,128)(4,1)S(1)} %copy-done.1, bf16[512,2,2,128]{0,3,2,1:T(8,128)(2,1)S(1)} %bitcast.88, bf16[2048,2,128]{2,0,1:T(8,128)(2,1)S(1)} %maximum_maximum_fusion), kind=kOutput, calls=%fused_computation.92 | convolution fusion | flops 821036544 | bytes 15474688 | tf_op jit(solution)/shard_map/sub | solution.py:47
  295.1 0.0 collective-permute-done
  295.1 6.2 %fusion.26 = bf16[2,128,2,512]{3,1,2,0:T(8,128)(2,1)S(1)} fusion(f32[2,2,512,1536]{2,3,1,0:T(8,128)} %get-tuple-element.24, f32[2,2,512]{2,1,0:T(2,128)S(1)} %get-tuple-element.23, bf16[1024,2,128]{0,2,1:T(8,128)(2,1)} %bitcast, bf16[1024,2,128]{0,2,1:T(8,128)(2,1)} %collective-permute-done), kind=kOutput, calls=%fused_computation.42 | convolution fusion | flops 813432832 | bytes 14163968 | tf_op jit(solution)/shard_map/hgrk,khd->rhgd/dot_general | solution.py:49
  301.4 2.6 copy-done.6
  304.0 2.2 fusion.27
  306.2 0.1 all-gather.14.cloned.1.call-done
  306.3 11.5 %convolution_convert_fusion = bf16[1024,5376]{1,0:T(8,128)(2,1)} fusion(bf16[512,5376]{0,1:T(8,128)(2,1)} %all-gather.14.cloned.1.call-done, bf16[512,512]{0,1:T(8,128)(2,1)S(1)} %bitcast.90, bf16[512,512]{0,1:T(8,128)(2,1)S(1)} %bitcast.91), kind=kOutput, calls=%fused_computation.8 | convolution fusion | flops 5644746752 | bytes 17563648 | tf_op jit(solution)/shard_map/dot_general | solution.py:117
  317.9 0.0 reduce-scatter.2.cloned.1.call-update
  317.9 137.5 %reduce-scatter.2.cloned.1.call-done = bf16[128,5376]{1,0:T(8,128)(2,1)} async-done(((bf16[1024,5376]{1,0:T(8,128)(2,1)}), bf16[128,5376]{1,0:T(8,128)(2,1)}) %reduce-scatter.2.cloned.1.call-update) | async-done | bytes 1376272 | tf_op jit(solution)/shard_map/reduce_scatter | solution.py:116
  455.4 1.7 fusion.16
  457.1 3.0 fusion.21
  (23 shorter events, 0.1 us)
Async XLA Ops:
  6.5 40.0 %all-gather.10.cloned.1.call-start = ((), (), s32[]{:S(2)}) async-start(), calls=%async_computation.3 | async-start | bytes 2924544 | tf_op jit(solution)/shard_map/all_gather | solution.py:104
  7.3 171.6 %all-gather.6.cloned.1.call-start = ((), (), s32[]{:S(2)}) async-start(), calls=%async_computation.1 | async-start | bytes 12386304 | tf_op jit(solution)/shard_map/all_gather | solution.py:96
  11.8 205.7 %all-gather.8.cloned.1.call-start = ((), (), s32[]{:S(2)}) async-start(), calls=%async_computation.2 | async-start | bytes 2924544 | tf_op jit(solution)/shard_map/all_gather | solution.py:105
  12.6 252.1 %all-gather.12.cloned.1.call-start = ((), (), s32[]{:S(2)}) async-start(), calls=%async_computation.4 | async-start | bytes 5849088 | tf_op jit(solution)/shard_map/all_gather | solution.py:103
  13.1 293.2 %all-gather.14.cloned.1.call-start = ((), (), s32[]{:S(2)}) async-start(), calls=%async_computation.5 | async-start | bytes 5849088 | tf_op jit(solution)/shard_map/all_gather | solution.py:115
  13.7 441.7 %reduce-scatter.2.cloned.1.call-start = ((), (), s32[]{:S(2)}) async-start(), calls=%async_computation.6 | async-start | bytes 12386304 | tf_op jit(solution)/shard_map/reduce_scatter | solution.py:116
  18.5 171.0 %copy-start.4 = (f32[128]{0:T(128)S(1)}, f32[128]{0:T(128)}, u32[]{:S(2)}) copy-start(f32[128]{0:T(128)} %param.16) | copy-start | bytes 1540
  191.4 85.6 %collective-permute-start.1 = (bf16[1024,2,128]{2,0,1:T(8,128)(2,1)}, bf16[1024,2,128]{2,0,1:T(8,128)(2,1)S(1)}, u32[]{:S(2)}, u32[]{:S(2)}) collective-permute-start(bf16[1024,2,128]{2,0,1:T(8,128)(2,1)} %pad_maximum_fusion.2), channel_id=1, source_target_pairs={{0,8},{8,16},{16,24},{24,32},{32,40},{40,48},{48,56},{56,64},{64,7... | collective-permute-start | bytes 1572872 | tf_op jit(solution)/shard_map/ppermute | solution.py:13
  226.3 48.7 %copy-start.5 = (f32[128]{0:T(128)S(1)}, f32[128]{0:T(128)}, u32[]{:S(2)}) copy-start(f32[128]{0:T(128)} %param.15) | copy-start | bytes 1540
  226.3 68.8 %collective-permute-start = (bf16[1024,2,128]{0,2,1:T(8,128)(2,1)}, bf16[1024,2,128]{0,2,1:T(8,128)(2,1)}, u32[]{:S(2)}, u32[]{:S(2)}) collective-permute-start(bf16[1024,2,128]{0,2,1:T(8,128)(2,1)} %bitcast), channel_id=1, source_target_pairs={{0,8},{8,16},{16,24},{24,32},{32,40},{40,48},{48,56},{56,64},{64,7... | collective-permute-start | bytes 1572872 | tf_op jit(solution)/shard_map/ppermute | solution.py:13
  277.3 9.5 %copy-start.1 = (pred[512,1536]{0,1:T(8,128)(4,1)S(1)}, pred[512,1536]{0,1:T(8,128)(4,1)}, u32[]{:S(2)}) copy-start(pred[512,1536]{0,1:T(8,128)(4,1)} %fusion.15) | copy-start | bytes 2359300
  277.3 9.5 %copy-start.2 = (bf16[512,4,128]{0,2,1:T(8,128)(2,1)S(1)}, bf16[512,4,128]{0,2,1:T(8,128)(2,1)}, u32[]{:S(2)}) copy-start(bf16[512,4,128]{0,2,1:T(8,128)(2,1)} %get-tuple-element.10) | copy-start | bytes 1572868
  295.1 8.9 %copy-start.6 = (f32[2,2,512,1536]{2,3,1,0:T(8,128)S(1)}, f32[2,2,512,1536]{2,3,1,0:T(8,128)}, u32[]{:S(2)}) copy-start(f32[2,2,512,1536]{2,3,1,0:T(8,128)} %get-tuple-element.26) | copy-start | bytes 37748740
  317.9 139.2 %copy-start = (bf16[128,5376]{1,0:T(8,128)(2,1)S(1)}, bf16[128,5376]{1,0:T(8,128)(2,1)}, u32[]{:S(2)}) copy-start(bf16[128,5376]{1,0:T(8,128)(2,1)} %param.9) | copy-start | bytes 4128772
  317.9 139.2 %copy-start.3 = (f32[5376]{0:T(1024)S(1)}, f32[5376]{0:T(1024)}, u32[]{:S(2)}) copy-start(f32[5376]{0:T(1024)} %param.17) | copy-start | bytes 64516
Sparse Core Ops, SparseCore 0:
  9.0 37.4 all-gather.9
  48.8 130.0 all-gather.5
  180.6 36.9 all-gather.7
  219.1 45.5 all-gather.11
  266.2 40.0 all-gather.13
  318.0 137.3 reduce-scatter.1
where the time goes:
time: 467 us
  waiting for transfers between devices  361 us (77%)
  matrix products  65.9 us (14%)
  other arithmetic  17.5 us (4%)
  between operations  13.7 us (3%)
    reduce_scatter x1, waiting for transfers between devices, per_device(): lax.psum_scatter(jnp.dot(attended, out_full, preferred_element_type=jnp.f...  138 us
    all_gather x1, waiting for transfers between devices, per_device(): block = lax.all_gather(normed, 'tp', axis=0, tiled=True)  132 us
    all_gather x1, waiting for transfers between devices, per_device(): lax.all_gather(query_weight, 'ctx', axis=0, tiled=True)  35.3 us
    dot_general x3, matrix products, add_product(): return jnp.dot(left, weight_piece, preferred_element_type=jnp.float32)  28.1 us
    all_gather x1, waiting for transfers between devices, per_device(): lax.all_gather(key_weight, 'ctx', axis=0, tiled=True)  28.1 us
    all_gather x1, waiting for transfers between devices, per_device(): lax.all_gather(value_weight, 'ctx', axis=0, tiled=True)  24.8 us
    sub x2, matrix products, attend(): expo = jnp.where(allowed, jnp.exp(scores - row_max), 0.0)  17.8 us
    dot_general x1, matrix products, per_device(): jnp.dot(attended, out_full, preferred_element_type=jnp.float32)  11.5 us
  transfers between devices with their start and end apart: 8, of which 6 were waited for; matrix products, arithmetic and copies ran while one was open for 15% of the time, Pallas kernels for 0%

commit v1 on v0

v1 whole, which is shorter than its diff:
```python
import functools

import jax
import jax.numpy as jnp
from jax import lax
from jax.experimental import pallas as pl
from jax.experimental.pallas import tpu as pltpu
from jax.sharding import PartitionSpec as P

WINDOW = 1024
SCALE = 168.0 ** (-0.5)
EPS = 1e-06
D = 5376
PIECE = 336
TOK = 512
HEAD = 128
KCH = 768
NK = D // KCH
TILE = 896
NT = D // TILE
MESH = pl.DeviceIdType.MESH
BF = jnp.bfloat16
F32 = jnp.float32

STEP_A = (-1, 1, 0, 0, 2, -1, -1, 1, 1, 0, -1, 2, 2, 1, 2)
STEP_B = (0, 0, -1, 1, 0, -1, 1, -1, 1, 2, 2, -1, 1, 2, 2)
NSTEP = 15


def pick(k, values):
    out = jnp.int32(values[-1])
    for i in range(len(values) - 2, -1, -1):
        if values[i] != values[-1]:
            out = jnp.where(k == i, jnp.int32(values[i]), out)
    return out


def among(k, values):
    hit = k == values[0]
    for v in values[1:]:
        hit = hit | (k == v)
    return hit


def kernel(
    hid_ref, ing_ref, wq_ref, wk_ref, wv_ref, wo_ref, cos_ref, sin_ref, qg_ref, kg_ref, pg_ref,
    out_ref,
    w, act, kv, q, att, acc, bias, relay, rbuf, proj,
    own_sem, ici_recv, part_recv, ici_send, part_send,
    act_recv, act_send, halo_recv, halo_send, relay_recv, rs_recv, rs_send,
):
    ctx = lax.axis_index("ctx")
    tp = lax.axis_index("tp")
    z, xl, c = ctx // 4, (ctx // 2) % 2, ctx % 2
    xh, y = tp // 4, tp % 4
    x = xh * 2 + xl
    block = (z * 2 + xl) * 4 + c * 2 + xh

    def dev(dx, dz, core, dy):
        xx, zz, yy = (x + dx + 4) % 4, (z + dz + 4) % 4, (y + dy + 4) % 4
        return (zz * 4 + (xx % 2) * 2 + core, (xx // 2) * 4 + yy)

    def block_dev(b):
        return ((b // 8) * 4 + ((b // 4) % 2) * 2 + (b // 2) % 2, (b % 2) * 4 + y)

    yp, ym = dev(0, 0, c, 1), dev(0, 0, c, -1)
    partner = dev(0, 0, 1 - c, 0)
    ahead = [block_dev((block + 1) % 32), block_dev((block + 2) % 32)]
    behind = [block_dev((block + 31) % 32), block_dev((block + 30) % 32)]

    barrier = pltpu.get_barrier_semaphore()
    peers = [dev(1, 0, c, 0), dev(-1, 0, c, 0), dev(0, 1, c, 0), dev(0, -1, c, 0), yp, ym, partner]
    peers += ahead + behind
    for peer in peers:
        pl.semaphore_signal(barrier, inc=1, device_id=peer, device_id_type=MESH)

    own_rows = pl.ds(pl.multiple_of(ctx * PIECE, 16), PIECE)
    loads = [
        pltpu.make_async_copy(wk_ref, w.at[0, xh, own_rows, pl.ds(0, 256)], own_sem.at[0]),
        pltpu.make_async_copy(wv_ref, w.at[0, xh, own_rows, pl.ds(256, 256)], own_sem.at[1]),
        pltpu.make_async_copy(wq_ref, w.at[1, xh, own_rows], own_sem.at[2]),
        pltpu.make_async_copy(wo_ref, w.at[2, xh, own_rows], own_sem.at[3]),
    ]
    for load in loads:
        load.start()

    def x_first(s):
        return c == 0

    def axis_dev(s, first, sign):
        along_x = x_first(s) if first else jnp.logical_not(x_first(s))
        dx = jnp.where(along_x, sign, 0)
        dz = jnp.where(along_x, 0, sign)
        return dev(dx, dz, c, 0)

    def piece(s, da, db):
        fx = x_first(s)
        dx, dz = jnp.where(fx, da, db), jnp.where(fx, db, da)
        xx, zz = (x + dx + 4) % 4, (z + dz + 4) % 4
        row = pl.multiple_of((zz * 4 + (xx % 2) * 2 + c) * PIECE, 16)
        return w.at[s, xx // 2, pl.ds(row, PIECE)]

    def send(s, ref, device, at):
        pltpu.make_async_remote_copy(
            src_ref=ref, dst_ref=ref, send_sem=ici_send.at[s], recv_sem=ici_recv.at[s, at],
            device_id=device, device_id_type=MESH,
        ).start()

    def send_partner(s, ref):
        pltpu.make_async_remote_copy(
            src_ref=ref, dst_ref=ref, send_sem=part_send.at[s], recv_sem=part_recv.at[s],
            device_id=partner, device_id_type=MESH,
        ).start()

    def start_own(s):
        ref = piece(s, 0, 0)
        send(s, ref, axis_dev(s, True, 1), 0)
        send(s, ref, axis_dev(s, True, -1), 1)
        send(s, ref, axis_dev(s, False, 1), 2)
        send(s, ref, axis_dev(s, False, -1), 3)
        send_partner(s, ref)

    def comm_step(g):
        s, k = g // NSTEP, g % NSTEP
        ref = piece(s, pick(k, STEP_A), pick(k, STEP_B))
        pltpu.make_async_copy(ref, ref, ici_recv.at[s, k]).wait()

        @pl.when(among(k, (0, 1, 4, 2, 7)))
        def _():
            send(s, ref, axis_dev(s, False, 1), pick(k, (5, 7, 9, 0, 11, 0, 0, 13)))

        @pl.when(among(k, (0, 1, 4, 6, 12)))
        def _():
            send(s, ref, axis_dev(s, False, -1), pick(k, (6, 8, 0, 0, 12, 0, 10, 0, 0, 0, 0, 0, 14)))

        @pl.when((k == 0) & (s % 2 == 0))
        def _():
            send(s, ref, axis_dev(s, True, 1), 4)

        @pl.when((k == 1) & (s % 2 == 1))
        def _():
            send(s, ref, axis_dev(s, True, -1), 4)

        send_partner(s, ref)

        @pl.when((k == 8) & (s < 2))
        def _():
            start_own(s + 1)

    def await_partner(s):
        pltpu.make_async_copy(w.at[s, 0], w.at[s, 0], part_recv.at[s]).wait()

    pl.semaphore_wait(barrier, len(peers))
    loads[0].wait()
    loads[1].wait()
    start_own(0)

    hid = hid_ref[...].astype(F32)
    mean = jnp.mean(hid * hid, axis=-1, keepdims=True)
    act[y] = (hid * lax.rsqrt(mean + EPS) * ing_ref[...]).astype(BF)
    loads[2].wait()
    loads[3].wait()

    def act_copy(owner, half, device, at):
        ref = act.at[owner, pl.ds(half * 64, 64)]
        return pltpu.make_async_remote_copy(
            src_ref=ref, dst_ref=ref, send_sem=act_send, recv_sem=act_recv.at[at],
            device_id=device, device_id_type=MESH,
        )

    act_copy(y, 0, yp, 0).start()
    act_copy(y, 1, ym, 3).start()
    act_copy(y, 1, yp, 1).start()
    act_copy(y, 0, ym, 2).start()
    before, after, across = (y + 3) % 4, (y + 1) % 4, (y + 2) % 4

    row = lax.broadcasted_iota(jnp.int32, (HEAD, 1152), 0)
    col = lax.broadcasted_iota(jnp.int32, (HEAD, 1152), 1)

    def mask_body(qc, carry):
        least = WINDOW - block * TOK - qc * 128
        allowed = (col > row) & (col <= row + WINDOW) & (col >= least)
        bias[qc] = jnp.where(allowed, 0.0, -1e30)
        return carry

    lax.fori_loop(0, 4, mask_body, 0)

    def stream_body(g, carry):
        comm_step(g)

        @pl.when(g == 8)
        def _():
            act_copy(before, 0, yp, 0).wait_recv()
            act_copy(before, 0, yp, 4).start()
            act_copy(after, 1, ym, 3).wait_recv()
            act_copy(after, 1, ym, 5).start()

        return carry

    lax.fori_loop(0, 22, stream_body, 0)
    act_copy(before, 1, yp, 1).wait_recv()
    act_copy(after, 0, ym, 2).wait_recv()
    act_copy(across, 0, yp, 4).wait_recv()
    act_copy(across, 1, ym, 5).wait_recv()
    await_partner(0)

    def project(s, j):
        half, kk = j // NK, j % NK
        left = act[:, :, pl.ds(pl.multiple_of(kk * KCH, KCH), KCH)].reshape(TOK, KCH)
        right = w[s, half, pl.ds(pl.multiple_of(kk * KCH, KCH), KCH), :]
        part = jnp.dot(left, right, preferred_element_type=F32)

        @pl.when(kk == 0)
        def _():
            acc[...] = part

        @pl.when(kk > 0)
        def _():
            acc[...] += part

    def normed_rope(vec, gain):
        mean = jnp.mean(vec * vec, axis=-1, keepdims=True)
        vec = vec * lax.rsqrt(mean + EPS) * gain
        return (vec * cos_ref[...] + pltpu.roll(vec, HEAD // 2, 1) * sin_ref[...]).astype(BF)

    def halo_copy(half, ahead_by):
        heads = pl.ds(half * 2, 2)
        return pltpu.make_async_remote_copy(
            src_ref=kv.at[:, heads, pl.ds(2 * TOK, TOK)],
            dst_ref=kv.at[:, heads, pl.ds((2 - ahead_by) * TOK, TOK)],
            send_sem=halo_send, recv_sem=halo_recv.at[ahead_by - 1, half],
            device_id=ahead[ahead_by - 1], device_id_type=MESH,
        )

    def kv_chunk(j):
        project(0, j)
        half = j // NK

        @pl.when(j % NK == NK - 1)
        def _():
            for h in range(2):
                kv[0, half * 2 + h, pl.ds(2 * TOK, TOK)] = normed_rope(
                    acc[:, h * HEAD : (h + 1) * HEAD], kg_ref[...]
                )
                kv[1, half * 2 + h, pl.ds(2 * TOK, TOK)] = acc[
                    :, (2 + h) * HEAD : (3 + h) * HEAD
                ].astype(BF)
            halo_copy(half, 1).start()
            halo_copy(half, 2).start()

    def q_chunk(j):
        project(1, j)
        half = j // NK

        @pl.when(j % NK == NK - 1)
        def _():
            for h in range(4):
                q[half * 2 + h // 2, h % 2] = normed_rope(
                    acc[:, h * HEAD : (h + 1) * HEAD], qg_ref[...]
                )

    def kv_body(j, carry):
        kv_chunk(j)

        @pl.when(j % 2 == 1)
        def _():
            comm_step(22 + j // 2)

        return carry

    lax.fori_loop(0, 2 * NK, kv_body, 0)
    comm_step(29)
    await_partner(1)

    def q_body(j, carry):
        q_chunk(j)

        @pl.when(j % 2 == 1)
        def _():
            comm_step(30 + j // 2)

        return carry

    lax.fori_loop(0, 2 * NK, q_body, 0)
    for half in range(2):
        halo_copy(half, 1).wait_recv()
        halo_copy(half, 2).wait_recv()

    def attend_body(it, carry):
        qc, kvh = it // 4, it % 4
        start = pl.multiple_of(qc * 128, 128)
        queries = q[kvh, :, pl.ds(start, 128), :].reshape(256, HEAD)
        keys = kv[0, kvh, pl.ds(start, 1152), :]
        values = kv[1, kvh, pl.ds(start, 1152), :]
        scores = lax.dot_general(
            queries, keys, (((1,), (1,)), ((), ())), preferred_element_type=F32
        )
        scores = scores.reshape(2, 128, 1152) * SCALE + bias[qc][None]
        expo = jnp.exp(scores - jnp.max(scores, axis=-1, keepdims=True))
        weights = (expo * (1.0 / jnp.sum(expo, axis=-1, keepdims=True))).astype(BF)
        mixed = jnp.dot(weights.reshape(256, 1152), values, preferred_element_type=F32).astype(BF)
        for h in range(2):
            lanes = pl.ds(pl.multiple_of((kvh % 2) * 256 + h * 128, 128), 128)
            att[kvh // 2, pl.ds(start, 128), lanes] = mixed[h * 128 : (h + 1) * 128]

        @pl.when(it % 2 == 1)
        def _():
            comm_step(37 + it // 2)

        return carry

    lax.fori_loop(0, 16, attend_body, 0)
    await_partner(2)
    pltpu.make_async_copy(act.at[pl.ds(0, 3)], act.at[pl.ds(0, 3)], act_send).wait()

    def lanes_of(n):
        return pl.ds(pl.multiple_of(n * TILE, 128), TILE)

    def relay_copy(n, device):
        return pltpu.make_async_remote_copy(
            src_ref=act.at[across, :, lanes_of(n)], dst_ref=relay.at[:, lanes_of(n)],
            send_sem=rs_send, recv_sem=relay_recv.at[n], device_id=device, device_id_type=MESH,
        )

    def sum_copy(n, chunk, side, device):
        return pltpu.make_async_remote_copy(
            src_ref=act.at[chunk, :, lanes_of(n)], dst_ref=rbuf.at[side, :, lanes_of(n)],
            send_sem=rs_send, recv_sem=rs_recv.at[side, n], device_id=device, device_id_type=MESH,
        )

    def out_body(n, carry):
        @pl.when(n < NT)
        def _():
            rows = pl.ds(pl.multiple_of(n * TILE, 128), TILE)
            part = lax.dot_general(
                att[0], w[2, 0, rows, :], (((1,), (1,)), ((), ())), preferred_element_type=F32
            )
            part += lax.dot_general(
                att[1], w[2, 1, rows, :], (((1,), (1,)), ((), ())), preferred_element_type=F32
            )
            act[:, :, lanes_of(n)] = part.astype(BF).reshape(4, 128, TILE)

            @pl.when(n % 2 == 0)
            def _():
                relay_copy(n, yp).start()
                sum_copy(n, before, 1, ym).start()

            @pl.when(n % 2 == 1)
            def _():
                relay_copy(n, ym).start()
                sum_copy(n, after, 0, yp).start()

        @pl.when(n > 0)
        def _():
            m = n - 1
            relay_copy(m, yp).wait_recv()
            chunk = jnp.where(m % 2 == 0, after, before)
            merged = act[chunk, :, lanes_of(m)].astype(F32) + relay[:, lanes_of(m)].astype(F32)
            act[chunk, :, lanes_of(m)] = merged.astype(BF)

            @pl.when(m % 2 == 0)
            def _():
                sum_copy(m, after, 0, yp).start()

            @pl.when(m % 2 == 1)
            def _():
                sum_copy(m, before, 1, ym).start()

        return carry

    lax.fori_loop(0, NT + 1, out_body, 0)

    def sum_body(n, total):
        sum_copy(n, after, 0, yp).wait_recv()
        sum_copy(n, before, 1, ym).wait_recv()
        value = (
            act[y, :, lanes_of(n)].astype(F32)
            + rbuf[0, :, lanes_of(n)].astype(F32)
            + rbuf[1, :, lanes_of(n)].astype(F32)
        )
        proj[:, lanes_of(n)] = value
        return total + jnp.sum(value * value, axis=-1, keepdims=True)

    total = lax.fori_loop(0, NT, sum_body, jnp.zeros((128, 1), F32))
    scale = lax.rsqrt(total * (1.0 / D) + EPS)
    out_ref[...] = (hid_ref[...].astype(F32) + proj[...] * scale * pg_ref[...]).astype(BF)

    for s in range(3):
        sent = w.at[s, 0, pl.ds(0, NSTEP * PIECE)]
        pltpu.make_async_copy(sent, sent, ici_send.at[s]).wait()
        pltpu.make_async_copy(w.at[s, 0], w.at[s, 0], part_send.at[s]).wait()
    halo = kv.at[:, :, pl.ds(0, 2 * TOK)]
    pltpu.make_async_copy(halo, halo, halo_send).wait()
    pltpu.make_async_copy(act.at[pl.ds(0, 3)], act.at[pl.ds(0, 3)], rs_send).wait()


def per_device(
    hidden_in, in_gain, query_weight, key_weight, value_weight, out_weight, q_gain, k_gain, post_gain
):
    ctx, tp = lax.axis_index("ctx"), lax.axis_index("tp")
    block = ctx * 2 + tp // 4
    positions = block * TOK + jnp.arange(TOK, dtype=jnp.int32)
    frequency = 10000.0 ** (-(jnp.arange(HEAD // 2, dtype=F32) * 2.0 / HEAD))
    angles = positions.astype(F32)[:, None] * frequency[None, :]
    cosine, sine = jnp.cos(angles), jnp.sin(angles)
    cos_table = jnp.concatenate([cosine, cosine], axis=-1)
    sin_table = jnp.concatenate([-sine, sine], axis=-1)
    vmem, hbm = pl.BlockSpec(memory_space=pltpu.VMEM), pl.BlockSpec(memory_space=pl.ANY)
    dma = pltpu.SemaphoreType.DMA
    return pl.pallas_call(
        kernel,
        out_shape=jax.ShapeDtypeStruct((128, D), BF),
        in_specs=[vmem, vmem, hbm, hbm, hbm, hbm, vmem, vmem, vmem, vmem, vmem],
        out_specs=vmem,
        scratch_shapes=[
            pltpu.VMEM((3, 2, D, 512), BF),
            pltpu.VMEM((4, 128, D), BF),
            pltpu.VMEM((2, 4, 3 * TOK, HEAD), BF),
            pltpu.VMEM((4, 2, TOK, HEAD), BF),
            pltpu.VMEM((2, TOK, 512), BF),
            pltpu.VMEM((TOK, 512), F32),
            pltpu.VMEM((4, 128, 1152), F32),
            pltpu.VMEM((128, D), BF),
            pltpu.VMEM((2, 128, D), BF),
            pltpu.VMEM((128, D), F32),
            dma((4,)), dma((3, NSTEP)), dma((3,)), dma((3,)), dma((3,)),
            dma((6,)), dma, dma((2, 2)), dma, dma((NT,)), dma((2, NT)), dma,
        ],
        compiler_params=pltpu.CompilerParams(
            collective_id=0, has_side_effects=True, vmem_limit_bytes=67043328
        ),
    )(
        hidden_in,
        in_gain.reshape(1, D),
        query_weight,
        key_weight,
        value_weight,
        out_weight.T,
        cos_table,
        sin_table,
        q_gain.reshape(1, HEAD),
        k_gain.reshape(1, HEAD),
        post_gain.reshape(1, D),
    )


def solution(mesh):
    in_specs = (
        P(("ctx", "tp"), None), P(), P("ctx", "tp"), P("ctx", "tp"), P("ctx", "tp"), P("tp", "ctx"),
        P(), P(), P(),
    )
    return jax.shard_map(
        per_device, mesh=mesh, in_specs=in_specs, out_specs=P(("ctx", "tp"), None), check_vma=False
    )
```

time: 467 us -> 200 us (0.43)
  waiting for transfers between devices: 361 us -> 0 us
  Pallas kernels: 0 us -> 191 us
  matrix products: 65.9 us -> 0 us
  other arithmetic: 17.5 us -> 2 us
  between operations: 13.7 us -> 0.02 us
    all_gather x5 -> x0, waiting for transfers between devices: 221 us -> none  [the longest x1 132 us: per_device(): block = lax.all_gather(normed, 'tp', axis=0, tiled=True)]
    pallas_call x0 -> x1, Pallas kernels: none -> 191 us  [per_device(): pl.pallas_call(kernel, out_shape=jax.ShapeDtypeStruct((128, D), BF), in_s...]
    reduce_scatter x1 -> x0, waiting for transfers between devices: 138 us -> none  [per_device(): lax.psum_scatter(jnp.dot(attended, out_full, preferred_element_type=jnp.f...]
    dot_general x6 -> x0, matrix products: 48.1 us -> none  [the longest x3 28.1 us: add_product(): return jnp.dot(left, weight_piece, preferred_element_type=jnp.float32)]
    sub x2 -> x0, matrix products: 17.8 us -> none  [attend(): expo = jnp.where(allowed, jnp.exp(scores - row_max), 0.0)]
    convert_element_type x2 -> x1, other arithmetic: 5.79 us -> 0.01 us  [per_device(): angles = positions.astype(F32)[:, None] * frequency[None, :]]
  transfers between devices with their start and end apart: 8 -> 0, of which waited for: 6 -> 0; matrix products, arithmetic and copies ran while one was open for 15% -> 0% of each run, Pallas kernels for 0% -> 0%
where the time goes in v1:
time: 200 us; the launch traced here: 198 us
  Pallas kernels  191 us (96%)
  local copies, waits for them, and re-layouts  5.21 us (3%)
  other arithmetic  2 us (1%)
    pallas_call x1, Pallas kernels, per_device(): pl.pallas_call(kernel, out_shape=jax.ShapeDtypeStruct((128, D), BF), in_s...  191 us

profile of v1, /device:TPU:0, one launch (start us, length us, event | category | flops | bytes accessed | tf_op | source)
XLA Modules:
  0.0 198.4 jit_solution(8055467001826886)
XLA Ops:
  0.0 1.4 reshape.23.ing_ref
  1.4 1.3 reshape.26.pg_ref
  2.7 1.0 fusion
  3.7 1.0 pad_maximum_fusion
  4.7 191.2 %shard_map.91 = bf16[128,5376]{1,0:T(8,128)(2,1)} custom-call(bf16[128,5376]{1,0:T(8,128)(2,1)} %hid_ref.1, f32[1,5376]{1,0:T(1,128)} %reshape.23.ing_ref, bf16[336,512]{1,0:T(8,128)(2,1)} %wq_ref.1, bf16[336,256]{1,0:T(8,128)(2,1)} %wk_ref.1, bf16[336,256]{1,0:T(8,128)(2,1)} %wv_ref.1, bf16[336,512]{1,0:T(8,128)(2,1)} %bitcast.3, ...), custom_call_target="tpu_custom_call" | custom-call | tf_op jit(solution)/shard_map/pallas_call | solution.py:410
  195.9 2.5 %copy.11 = bf16[128,5376]{1,0:T(8,128)(2,1)} copy(bf16[128,5376]{1,0:T(8,128)(2,1)} %shard_map.91) | data formatting | bytes 2752512
  (2 shorter events, 0.0 us)

commit v2 on v1

--- a/solution.py
+++ b/solution.py
@@ -16,8 +16,8 @@
 HEAD = 128
 KCH = 768
 NK = D // KCH
-TILE = 896
-NT = D // TILE
+NT = 16
+LAG = 2
 MESH = pl.DeviceIdType.MESH
 BF = jnp.bfloat16
 F32 = jnp.float32
@@ -25,6 +25,8 @@
 STEP_A = (-1, 1, 0, 0, 2, -1, -1, 1, 1, 0, -1, 2, 2, 1, 2)
 STEP_B = (0, 0, -1, 1, 0, -1, 1, -1, 1, 2, 2, -1, 1, 2, 2)
 NSTEP = 15
+Q_ORDER = (0, 2, 6, 1, 4, 3, 5, 2, 0, 4, 1, 3, 6, 5, 4, 2, 6, 3, 5, 0, 1, 6, 4, 0, 5, 2, 1, 3)
+LOG2E = 1.4426950408889634
 
 
 def pick(k, values):
@@ -85,7 +87,7 @@
         load.start()
 
     def x_first(s):
-        return c == 0
+        return (c == 0) | (s == 1)
 
     def axis_dev(s, first, sign):
         along_x = x_first(s) if first else jnp.logical_not(x_first(s))
@@ -106,9 +108,11 @@
             device_id=device, device_id_type=MESH,
         ).start()
 
-    def send_partner(s, ref):
+    def send_partner(s, ref, k):
+        late = jnp.where((s == 1) & (k > 12) & (k < NSTEP), 1, 0)
         pltpu.make_async_remote_copy(
-            src_ref=ref, dst_ref=ref, send_sem=part_send.at[s], recv_sem=part_recv.at[s],
+            src_ref=ref, dst_ref=ref, send_sem=part_send.at[s],
+            recv_sem=part_recv.at[s, jnp.where(s == 2, k, late)],
             device_id=partner, device_id_type=MESH,
         ).start()
 
@@ -118,7 +122,7 @@
         send(s, ref, axis_dev(s, True, -1), 1)
         send(s, ref, axis_dev(s, False, 1), 2)
         send(s, ref, axis_dev(s, False, -1), 3)
-        send_partner(s, ref)
+        send_partner(s, ref, NSTEP)
 
     def comm_step(g):
         s, k = g // NSTEP, g % NSTEP
@@ -141,14 +145,15 @@
         def _():
             send(s, ref, axis_dev(s, True, -1), 4)
 
-        send_partner(s, ref)
+        send_partner(s, ref, k)
 
         @pl.when((k == 8) & (s < 2))
         def _():
             start_own(s + 1)
 
-    def await_partner(s):
-        pltpu.make_async_copy(w.at[s, 0], w.at[s, 0], part_recv.at[s]).wait()
+    def await_partner(s, at, count):
+        ref = w.at[s, 0, pl.ds(0, count * PIECE)]
+        pltpu.make_async_copy(ref, ref, part_recv.at[s, at]).wait()
 
     pl.semaphore_wait(barrier, len(peers))
     loads[0].wait()
@@ -197,26 +202,25 @@
 
         return carry
 
-    lax.fori_loop(0, 22, stream_body, 0)
+    lax.fori_loop(0, 19, stream_body, 0)
     act_copy(before, 1, yp, 1).wait_recv()
     act_copy(after, 0, ym, 2).wait_recv()
     act_copy(across, 0, yp, 4).wait_recv()
     act_copy(across, 1, ym, 5).wait_recv()
-    await_partner(0)
-
-    def project(s, j):
-        half, kk = j // NK, j % NK
-        left = act[:, :, pl.ds(pl.multiple_of(kk * KCH, KCH), KCH)].reshape(TOK, KCH)
-        right = w[s, half, pl.ds(pl.multiple_of(kk * KCH, KCH), KCH), :]
-        part = jnp.dot(left, right, preferred_element_type=F32)
-
-        @pl.when(kk == 0)
-        def _():
-            acc[...] = part
-
-        @pl.when(kk > 0)
-        def _():
-            acc[...] += part
+    await_partner(0, 0, 16)
+
+    def project(s, half, kk, first):
+        rows = pl.ds(pl.multiple_of(kk * KCH, KCH), KCH)
+        left = act[:, :, rows].reshape(TOK, KCH)
+        part = jnp.dot(left, w[s, half, rows, :], preferred_element_type=F32)
+
+        @pl.when(first)
+        def _():
+            acc[half] = part
+
+        @pl.when(jnp.logical_not(first))
+        def _():
+            acc[half] += part
 
     def normed_rope(vec, gain):
         mean = jnp.mean(vec * vec, axis=-1, keepdims=True)
@@ -232,52 +236,55 @@
             device_id=ahead[ahead_by - 1], device_id_type=MESH,
         )
 
-    def kv_chunk(j):
-        project(0, j)
-        half = j // NK
-
-        @pl.when(j % NK == NK - 1)
+    def kv_body(j, carry):
+        half, kk = j // NK, j % NK
+        project(0, half, kk, kk == 0)
+
+        @pl.when(kk == NK - 1)
         def _():
             for h in range(2):
                 kv[0, half * 2 + h, pl.ds(2 * TOK, TOK)] = normed_rope(
-                    acc[:, h * HEAD : (h + 1) * HEAD], kg_ref[...]
+                    acc[half, :, h * HEAD : (h + 1) * HEAD], kg_ref[...]
                 )
                 kv[1, half * 2 + h, pl.ds(2 * TOK, TOK)] = acc[
-                    :, (2 + h) * HEAD : (3 + h) * HEAD
+                    half, :, (2 + h) * HEAD : (3 + h) * HEAD
                 ].astype(BF)
             halo_copy(half, 1).start()
             halo_copy(half, 2).start()
 
-    def q_chunk(j):
-        project(1, j)
-        half = j // NK
-
-        @pl.when(j % NK == NK - 1)
+        @pl.when(j % 4 == 3)
+        def _():
+            comm_step(19 + j // 4)
+
+        return carry
+
+    def step_body(g, carry):
+        comm_step(g)
+        return carry
+
+    lax.fori_loop(0, 2 * NK, kv_body, 0)
+    lax.fori_loop(22, 28, step_body, 0)
+    await_partner(1, 0, 14)
+
+    def q_body(j, carry):
+        half, p = j % 2, j // 2
+
+        @pl.when(j == 8)
+        def _():
+            await_partner(1, 1, 2)
+
+        project(1, half, pick(z * NK + p, Q_ORDER), p == 0)
+
+        @pl.when(p == NK - 1)
         def _():
             for h in range(4):
                 q[half * 2 + h // 2, h % 2] = normed_rope(
-                    acc[:, h * HEAD : (h + 1) * HEAD], qg_ref[...]
+                    acc[half, :, h * HEAD : (h + 1) * HEAD], qg_ref[...]
                 )
 
-    def kv_body(j, carry):
-        kv_chunk(j)
-
-        @pl.when(j % 2 == 1)
-        def _():
-            comm_step(22 + j // 2)
-
-        return carry
-
-    lax.fori_loop(0, 2 * NK, kv_body, 0)
-    comm_step(29)
-    await_partner(1)
-
-    def q_body(j, carry):
-        q_chunk(j)
-
-        @pl.when(j % 2 == 1)
-        def _():
-            comm_step(30 + j // 2)
+        @pl.when((j == 3) | (j == 7) | (j == 9) | (j == 11) | (j == 13))
+        def _():
+            comm_step(pick(j // 2, (0, 28, 0, 29, 30, 31, 32)))
 
         return carry
 
@@ -286,8 +293,7 @@
         halo_copy(half, 1).wait_recv()
         halo_copy(half, 2).wait_recv()
 
-    def attend_body(it, carry):
-        qc, kvh = it // 4, it % 4
+    def attend(rel, qc, kvh):
         start = pl.multiple_of(qc * 128, 128)
         queries = q[kvh, :, pl.ds(start, 128), :].reshape(256, HEAD)
         keys = kv[0, kvh, pl.ds(start, 1152), :]
@@ -295,103 +301,138 @@
         scores = lax.dot_general(
             queries, keys, (((1,), (1,)), ((), ())), preferred_element_type=F32
         )
-        scores = scores.reshape(2, 128, 1152) * SCALE + bias[qc][None]
-        expo = jnp.exp(scores - jnp.max(scores, axis=-1, keepdims=True))
+        scores = scores.reshape(2, 128, 1152) * (SCALE * LOG2E) + bias[qc][None]
+        expo = jnp.exp2(scores - jnp.max(scores, axis=-1, keepdims=True))
         weights = (expo * (1.0 / jnp.sum(expo, axis=-1, keepdims=True))).astype(BF)
         mixed = jnp.dot(weights.reshape(256, 1152), values, preferred_element_type=F32).astype(BF)
+        rows = pl.ds(pl.multiple_of(rel * 128, 128), 128)
         for h in range(2):
             lanes = pl.ds(pl.multiple_of((kvh % 2) * 256 + h * 128, 128), 128)
-            att[kvh // 2, pl.ds(start, 128), lanes] = mixed[h * 128 : (h + 1) * 128]
-
-        @pl.when(it % 2 == 1)
-        def _():
-            comm_step(37 + it // 2)
-
-        return carry
-
-    lax.fori_loop(0, 16, attend_body, 0)
-    await_partner(2)
-    pltpu.make_async_copy(act.at[pl.ds(0, 3)], act.at[pl.ds(0, 3)], act_send).wait()
-
-    def lanes_of(n):
-        return pl.ds(pl.multiple_of(n * TILE, 128), TILE)
+            att[kvh // 2, rows, lanes] = mixed[h * 128 : (h + 1) * 128]
+
+    def attend_body(it, carry):
+        rel, pair = it // 2, it % 2
+        qc = (y + pick(rel, (2, 1, 3, 0))) % 4
+        attend(rel, qc, pair * 2)
+        attend(rel, qc, pair * 2 + 1)
+        comm_step(33 + it)
+        return carry
+
+    lax.fori_loop(0, 8, attend_body, 0)
+    sent = w.at[0, 0, pl.ds(0, NSTEP * PIECE)]
+    pltpu.make_async_copy(sent, sent, ici_send.at[0]).wait()
+    pltpu.make_async_copy(w.at[0, 0], w.at[0, 0], part_send.at[0]).wait()
+
+    def tile_of(n):
+        u, mine = n // 2, n % 2 == 0
+        by_x = jnp.where(mine, c, 1 - c) == 0
+        other = jnp.where(by_x, pick(u, (1, 0, 1, 1, 0, 0, 1, 0)), pick(u, (1, 1, 1, 0, 0, 1, 0, 0)))
+        dz = jnp.where(by_x, pick(u, (0, 0, 3, 1, 3, 1, 2, 2)), pick(u, (0, 3, 1, 0, 3, 2, 1, 2)))
+        core = jnp.where(mine, c, 1 - c)
+        return ((z + dz) % 4) * 4 + ((xl + other) % 2) * 2 + core
+
+    def tile_rows(n):
+        return pl.ds(pl.multiple_of(tile_of(n) * PIECE, 16), PIECE)
 
     def relay_copy(n, device):
+        rows = tile_rows(n)
         return pltpu.make_async_remote_copy(
-            src_ref=act.at[across, :, lanes_of(n)], dst_ref=relay.at[:, lanes_of(n)],
+            src_ref=w.at[0, 0, rows, pl.ds(0, 128)], dst_ref=relay.at[rows],
             send_sem=rs_send, recv_sem=relay_recv.at[n], device_id=device, device_id_type=MESH,
         )
 
-    def sum_copy(n, chunk, side, device):
+    def sum_copy(n, rel, side, device):
+        rows = tile_rows(n)
         return pltpu.make_async_remote_copy(
-            src_ref=act.at[chunk, :, lanes_of(n)], dst_ref=rbuf.at[side, :, lanes_of(n)],
+            src_ref=w.at[0, 0, rows, pl.ds(rel * 128, 128)], dst_ref=rbuf.at[side, rows],
             send_sem=rs_send, recv_sem=rs_recv.at[side, n], device_id=device, device_id_type=MESH,
         )
 
     def out_body(n, carry):
+        @pl.when((n % 2 == 0) & (n >= 8) & (n < NT))
+        def _():
+            comm_step(37 + n // 2)
+
+        @pl.when((n % 2 == 1) & (n < NT))
+        def _():
+            u = n // 2
+            by_x = c == 1
+            one = jnp.where(by_x, pick(u, (0, 15, 5, 6, 2, 3, 10, 9)), pick(u, (2, 5, 7, 15, 0, 11, 1, 4)))
+            two = jnp.where(by_x, pick(u, (1, 4, 7, 8, 11, 12, 13, 14)), pick(u, (3, 6, 8, 9, 10, 12, 13, 14)))
+            await_partner(2, one, 1)
+            await_partner(2, two, 1)
+
         @pl.when(n < NT)
         def _():
-            rows = pl.ds(pl.multiple_of(n * TILE, 128), TILE)
-            part = lax.dot_general(
-                att[0], w[2, 0, rows, :], (((1,), (1,)), ((), ())), preferred_element_type=F32
-            )
-            part += lax.dot_general(
-                att[1], w[2, 1, rows, :], (((1,), (1,)), ((), ())), preferred_element_type=F32
-            )
-            act[:, :, lanes_of(n)] = part.astype(BF).reshape(4, 128, TILE)
+            rows = tile_rows(n)
+            dims = (((1,), (1,)), ((), ()))
+            part = lax.dot_general(w[2, 0, rows, :], att[0], dims, preferred_element_type=F32)
+            part += lax.dot_general(w[2, 1, rows, :], att[1], dims, preferred_element_type=F32)
+            w[0, 0, rows, :] = part.astype(BF)
 
             @pl.when(n % 2 == 0)
             def _():
                 relay_copy(n, yp).start()
-                sum_copy(n, before, 1, ym).start()
+                sum_copy(n, 2, 1, ym).start()
 
             @pl.when(n % 2 == 1)
             def _():
                 relay_copy(n, ym).start()
-                sum_copy(n, after, 0, yp).start()
-
-        @pl.when(n > 0)
-        def _():
-            m = n - 1
+                sum_copy(n, 1, 0, yp).start()
+
+        @pl.when(n >= LAG)
+        def _():
+            m = n - LAG
+            rows = tile_rows(m)
             relay_copy(m, yp).wait_recv()
-            chunk = jnp.where(m % 2 == 0, after, before)
-            merged = act[chunk, :, lanes_of(m)].astype(F32) + relay[:, lanes_of(m)].astype(F32)
-            act[chunk, :, lanes_of(m)] = merged.astype(BF)
 
             @pl.when(m % 2 == 0)
             def _():
-                sum_copy(m, after, 0, yp).start()
+                merged = w[0, 0, rows, pl.ds(128, 128)].astype(F32) + relay[rows].astype(F32)
+                w[0, 0, rows, pl.ds(128, 128)] = merged.astype(BF)
+                sum_copy(m, 1, 0, yp).start()
 
             @pl.when(m % 2 == 1)
             def _():
-                sum_copy(m, before, 1, ym).start()
-
-        return carry
-
-    lax.fori_loop(0, NT + 1, out_body, 0)
+                merged = w[0, 0, rows, pl.ds(256, 128)].astype(F32) + relay[rows].astype(F32)
+                w[0, 0, rows, pl.ds(256, 128)] = merged.astype(BF)
+                sum_copy(m, 2, 1, ym).start()
+
+        return carry
+
+    lax.fori_loop(0, NT + LAG, out_body, 0)
 
     def sum_body(n, total):
-        sum_copy(n, after, 0, yp).wait_recv()
-        sum_copy(n, before, 1, ym).wait_recv()
+        rows = tile_rows(n)
+        sum_copy(n, 1, 0, yp).wait_recv()
+        sum_copy(n, 2, 1, ym).wait_recv()
         value = (
-            act[y, :, lanes_of(n)].astype(F32)
-            + rbuf[0, :, lanes_of(n)].astype(F32)
-            + rbuf[1, :, lanes_of(n)].astype(F32)
-        )
-        proj[:, lanes_of(n)] = value
-        return total + jnp.sum(value * value, axis=-1, keepdims=True)
-
-    total = lax.fori_loop(0, NT, sum_body, jnp.zeros((128, 1), F32))
+            w[0, 0, rows, pl.ds(384, 128)].astype(F32)
+            + rbuf[0, rows].astype(F32)
+            + rbuf[1, rows].astype(F32)
+        )
+        padded = jnp.concatenate([value, jnp.zeros((48, 128), F32)], axis=0)
+        proj[tile_of(n)] = padded.T
+        return total + jnp.sum(value * value, axis=0, keepdims=True)
+
+    total = lax.fori_loop(0, NT, sum_body, jnp.zeros((1, 128), F32))
     scale = lax.rsqrt(total * (1.0 / D) + EPS)
-    out_ref[...] = (hid_ref[...].astype(F32) + proj[...] * scale * pg_ref[...]).astype(BF)
-
-    for s in range(3):
+    scale = jnp.broadcast_to(scale, (128, 128)).T[:, 0:1]
+    for t in range(NT):
+        cols = slice(t * PIECE, (t + 1) * PIECE)
+        out_ref[:, cols] = (
+            hid_ref[:, cols].astype(F32) + proj[t][:, :PIECE] * scale * pg_ref[:, cols]
+        ).astype(BF)
+
+    for s in (1, 2):
         sent = w.at[s, 0, pl.ds(0, NSTEP * PIECE)]
         pltpu.make_async_copy(sent, sent, ici_send.at[s]).wait()
         pltpu.make_async_copy(w.at[s, 0], w.at[s, 0], part_send.at[s]).wait()
     halo = kv.at[:, :, pl.ds(0, 2 * TOK)]
     pltpu.make_async_copy(halo, halo, halo_send).wait()
-    pltpu.make_async_copy(act.at[pl.ds(0, 3)], act.at[pl.ds(0, 3)], rs_send).wait()
+    summed = act.at[pl.ds(0, 3)]
+    pltpu.make_async_copy(summed, summed, rs_send).wait()
+    pltpu.make_async_copy(summed, summed, act_send).wait()
 
 
 def per_device(
@@ -418,12 +459,12 @@
             pltpu.VMEM((2, 4, 3 * TOK, HEAD), BF),
             pltpu.VMEM((4, 2, TOK, HEAD), BF),
             pltpu.VMEM((2, TOK, 512), BF),
-            pltpu.VMEM((TOK, 512), F32),
+            pltpu.VMEM((2, TOK, 512), F32),
             pltpu.VMEM((4, 128, 1152), F32),
-            pltpu.VMEM((128, D), BF),
-            pltpu.VMEM((2, 128, D), BF),
-            pltpu.VMEM((128, D), F32),
-            dma((4,)), dma((3, NSTEP)), dma((3,)), dma((3,)), dma((3,)),
+            pltpu.VMEM((D, 128), BF),
+            pltpu.VMEM((2, D, 128), BF),
+            pltpu.VMEM((NT, 128, 384), F32),
+            dma((4,)), dma((3, NSTEP)), dma((3, NSTEP + 1)), dma((3,)), dma((3,)),
             dma((6,)), dma, dma((2, 2)), dma, dma((NT,)), dma((2, NT)), dma,
         ],
         compiler_params=pltpu.CompilerParams(

time: 200 us -> 196 us (0.980)
  Pallas kernels: 191 us -> 186 us
    pallas_call x1, Pallas kernels: 191 us -> 186 us  [per_device(): pl.pallas_call(kernel, out_shape=jax.ShapeDtypeStruct((128, D), BF), in_s...]
where the time goes in v2:
time: 196 us; the launch traced here: 193 us
  Pallas kernels  186 us (95%)
  local copies, waits for them, and re-layouts  5.21 us (3%)
  other arithmetic  2 us (1%)
    pallas_call x1, Pallas kernels, per_device(): pl.pallas_call(kernel, out_shape=jax.ShapeDtypeStruct((128, D), BF), in_s...  186 us

profile of v2, /device:TPU:0, one launch (start us, length us, event | category | flops | bytes accessed | tf_op | source)
XLA Modules:
  0.0 193.1 jit_solution(1190368113164565597)
XLA Ops:
  0.0 1.4 reshape.23.ing_ref
  1.4 1.3 reshape.26.pg_ref
  2.7 1.0 fusion
  3.7 1.0 pad_maximum_fusion
  4.7 185.9 %shard_map.91 = bf16[128,5376]{1,0:T(8,128)(2,1)} custom-call(bf16[128,5376]{1,0:T(8,128)(2,1)} %hid_ref.1, f32[1,5376]{1,0:T(1,128)} %reshape.23.ing_ref, bf16[336,512]{1,0:T(8,128)(2,1)} %wq_ref.1, bf16[336,256]{1,0:T(8,128)(2,1)} %wk_ref.1, bf16[336,256]{1,0:T(8,128)(2,1)} %wv_ref.1, bf16[336,512]{1,0:T(8,128)(2,1)} %bitcast.3, ...), custom_call_target="tpu_custom_call" | custom-call | tf_op jit(solution)/shard_map/pallas_call | solution.py:451
  190.6 2.5 %copy.11 = bf16[128,5376]{1,0:T(8,128)(2,1)} copy(bf16[128,5376]{1,0:T(8,128)(2,1)} %shard_map.91) | data formatting | bytes 2752512
  (2 shorter events, 0.0 us)

commit v3 on v2

--- a/solution.py
+++ b/solution.py
@@ -17,7 +17,7 @@
 KCH = 768
 NK = D // KCH
 NT = 16
-LAG = 2
+SUM_AT = 20
 MESH = pl.DeviceIdType.MESH
 BF = jnp.bfloat16
 F32 = jnp.float32
@@ -25,7 +25,15 @@
 STEP_A = (-1, 1, 0, 0, 2, -1, -1, 1, 1, 0, -1, 2, 2, 1, 2)
 STEP_B = (0, 0, -1, 1, 0, -1, 1, -1, 1, 2, 2, -1, 1, 2, 2)
 NSTEP = 15
+OUT_START = 12
+KV_STEPS = (0, 0, 0, 19, 0, 0, 0, 20, 0, 0, 0, 21, 0, 0)
+KV_END = 22
+HALO_AT = 27
+Q_STEPS = (0, 0, 0, 0, 0, 0, 0, 30, 0, 31, 0, 32, 0, 33)
+ATT_START = 34
+GROUP = 8
 Q_ORDER = (0, 2, 6, 1, 4, 3, 5, 2, 0, 4, 1, 3, 6, 5, 4, 2, 6, 3, 5, 0, 1, 6, 4, 0, 5, 2, 1, 3)
+Q_OTHER = (0, 6, 1, 2, 3, 4, 5, 2, 0, 1, 3, 4, 5, 6, 4, 2, 3, 0, 1, 5, 6, 6, 4, 5, 0, 1, 2, 3)
 LOG2E = 1.4426950408889634
 
 
@@ -47,8 +55,8 @@
 def kernel(
     hid_ref, ing_ref, wq_ref, wk_ref, wv_ref, wo_ref, cos_ref, sin_ref, qg_ref, kg_ref, pg_ref,
     out_ref,
-    w, act, kv, q, att, acc, bias, relay, rbuf, proj,
-    own_sem, ici_recv, part_recv, ici_send, part_send,
+    w, act, kv, q, att, acc, bias, relay, rbuf, proj, squares,
+    own_sem, ici_recv, part_recv, ici_send, pass_send, part_send,
     act_recv, act_send, halo_recv, halo_send, relay_recv, rs_recv, rs_send,
 ):
     ctx = lax.axis_index("ctx")
@@ -87,10 +95,10 @@
         load.start()
 
     def x_first(s):
-        return (c == 0) | (s == 1)
+        return c == 0
 
     def axis_dev(s, first, sign):
-        along_x = x_first(s) if first else jnp.logical_not(x_first(s))
+        along_x = x_first(s) == first
         dx = jnp.where(along_x, sign, 0)
         dz = jnp.where(along_x, 0, sign)
         return dev(dx, dz, c, 0)
@@ -102,9 +110,9 @@
         row = pl.multiple_of((zz * 4 + (xx % 2) * 2 + c) * PIECE, 16)
         return w.at[s, xx // 2, pl.ds(row, PIECE)]
 
-    def send(s, ref, device, at):
+    def send(s, ref, device, at, sem):
         pltpu.make_async_remote_copy(
-            src_ref=ref, dst_ref=ref, send_sem=ici_send.at[s], recv_sem=ici_recv.at[s, at],
+            src_ref=ref, dst_ref=ref, send_sem=sem, recv_sem=ici_recv.at[s, at],
             device_id=device, device_id_type=MESH,
         ).start()
 
@@ -118,36 +126,42 @@
 
     def start_own(s):
         ref = piece(s, 0, 0)
-        send(s, ref, axis_dev(s, True, 1), 0)
-        send(s, ref, axis_dev(s, True, -1), 1)
-        send(s, ref, axis_dev(s, False, 1), 2)
-        send(s, ref, axis_dev(s, False, -1), 3)
+        send(s, ref, axis_dev(s, True, 1), 0, ici_send.at[s])
+        send(s, ref, axis_dev(s, True, -1), 1, ici_send.at[s])
+        send(s, ref, axis_dev(s, False, 1), 2, ici_send.at[s])
+        send(s, ref, axis_dev(s, False, -1), 3, ici_send.at[s])
         send_partner(s, ref, NSTEP)
+
+    def goes_plus(s, k):
+        return jnp.where(k < 2, s % 2 == 0, among(k, (2, 3, 7, 8)))
+
+    def passes_on(s, k):
+        plus = goes_plus(s, k)
+        up = among(k, (0, 2, 5, 7, 11)) & plus
+        down = among(k, (1, 3, 6, 8, 12)) & jnp.logical_not(plus)
+        return up, down
 
     def comm_step(g):
         s, k = g // NSTEP, g % NSTEP
         ref = piece(s, pick(k, STEP_A), pick(k, STEP_B))
         pltpu.make_async_copy(ref, ref, ici_recv.at[s, k]).wait()
 
-        @pl.when(among(k, (0, 1, 4, 2, 7)))
-        def _():
-            send(s, ref, axis_dev(s, False, 1), pick(k, (5, 7, 9, 0, 11, 0, 0, 13)))
-
-        @pl.when(among(k, (0, 1, 4, 6, 12)))
-        def _():
-            send(s, ref, axis_dev(s, False, -1), pick(k, (6, 8, 0, 0, 12, 0, 10, 0, 0, 0, 0, 0, 14)))
-
-        @pl.when((k == 0) & (s % 2 == 0))
-        def _():
-            send(s, ref, axis_dev(s, True, 1), 4)
-
-        @pl.when((k == 1) & (s % 2 == 1))
-        def _():
-            send(s, ref, axis_dev(s, True, -1), 4)
+        @pl.when(among(k, (0, 1, 4)))
+        def _():
+            at = pick(k, (5, 7, 0, 0, 11))
+            send(s, ref, axis_dev(s, False, 1), at, ici_send.at[s])
+            send(s, ref, axis_dev(s, False, -1), at + 1, ici_send.at[s])
+
+        up, down = passes_on(s, k)
+
+        @pl.when(up | down)
+        def _():
+            at = pick(k, (4, 4, 9, 9, 0, 10, 10, 13, 13, 0, 0, 14, 14))
+            send(s, ref, axis_dev(s, k < 2, jnp.where(up, 1, -1)), at, pass_send.at[s, k])
 
         send_partner(s, ref, k)
 
-        @pl.when((k == 8) & (s < 2))
+        @pl.when(((k == 8) & (s == 0)) | ((k == OUT_START) & (s == 1)))
         def _():
             start_own(s + 1)
 
@@ -249,31 +263,42 @@
                 kv[1, half * 2 + h, pl.ds(2 * TOK, TOK)] = acc[
                     half, :, (2 + h) * HEAD : (3 + h) * HEAD
                 ].astype(BF)
-            halo_copy(half, 1).start()
-            halo_copy(half, 2).start()
-
-        @pl.when(j % 4 == 3)
-        def _():
-            comm_step(19 + j // 4)
+
+        step = pick(j, KV_STEPS)
+
+        @pl.when(step > 0)
+        def _():
+            comm_step(step)
 
         return carry
 
     def step_body(g, carry):
         comm_step(g)
+
+        @pl.when(g == HALO_AT)
+        def _():
+            for half in range(2):
+                halo_copy(half, 1).start()
+                halo_copy(half, 2).start()
+
         return carry
 
     lax.fori_loop(0, 2 * NK, kv_body, 0)
-    lax.fori_loop(22, 28, step_body, 0)
+    lax.fori_loop(KV_END, 28, step_body, 0)
     await_partner(1, 0, 14)
 
     def q_body(j, carry):
-        half, p = j % 2, j // 2
-
-        @pl.when(j == 8)
-        def _():
+        mine = (j < 4) | ((j >= 6) & (j < 9))
+        half = jnp.where(mine, xh, 1 - xh)
+        p = pick(j, (0, 1, 2, 3, 0, 1, 4, 5, 6, 2, 3, 4, 5, 6))
+        order = jnp.where(mine, pick(z * NK + p, Q_ORDER), pick(z * NK + p, Q_OTHER))
+
+        @pl.when(j == 6)
+        def _():
+            lax.fori_loop(28, 30, step_body, 0)
             await_partner(1, 1, 2)
 
-        project(1, half, pick(z * NK + p, Q_ORDER), p == 0)
+        project(1, half, order, p == 0)
 
         @pl.when(p == NK - 1)
         def _():
@@ -282,13 +307,16 @@
                     acc[half, :, h * HEAD : (h + 1) * HEAD], qg_ref[...]
                 )
 
-        @pl.when((j == 3) | (j == 7) | (j == 9) | (j == 11) | (j == 13))
-        def _():
-            comm_step(pick(j // 2, (0, 28, 0, 29, 30, 31, 32)))
+        step = pick(j, Q_STEPS)
+
+        @pl.when(step > 0)
+        def _():
+            comm_step(step)
 
         return carry
 
     lax.fori_loop(0, 2 * NK, q_body, 0)
+    lax.fori_loop(34, ATT_START, step_body, 0)
     for half in range(2):
         halo_copy(half, 1).wait_recv()
         halo_copy(half, 2).wait_recv()
@@ -310,18 +338,36 @@
             lanes = pl.ds(pl.multiple_of((kvh % 2) * 256 + h * 128, 128), 128)
             att[kvh // 2, rows, lanes] = mixed[h * 128 : (h + 1) * 128]
 
-    def attend_body(it, carry):
+    def attend_step(it):
         rel, pair = it // 2, it % 2
-        qc = (y + pick(rel, (2, 1, 3, 0))) % 4
+        qc = (y + pick(rel, (2, 0, 1, 3))) % 4
         attend(rel, qc, pair * 2)
         attend(rel, qc, pair * 2 + 1)
-        comm_step(33 + it)
-        return carry
-
-    lax.fori_loop(0, 8, attend_body, 0)
-    sent = w.at[0, 0, pl.ds(0, NSTEP * PIECE)]
-    pltpu.make_async_copy(sent, sent, ici_send.at[0]).wait()
-    pltpu.make_async_copy(w.at[0, 0], w.at[0, 0], part_send.at[0]).wait()
+
+    def attend_body(it, carry):
+        attend_step(it)
+        comm_step(ATT_START + it)
+        return carry
+
+    lax.fori_loop(0, 4, attend_body, 0)
+    def drain(s):
+        sent = w.at[s, 0, pl.ds(0, 10 * PIECE)]
+        pltpu.make_async_copy(sent, sent, ici_send.at[s]).wait()
+        pltpu.make_async_copy(w.at[s, 0], w.at[s, 0], part_send.at[s]).wait()
+
+        def drain_body(k, carry):
+            up, down = passes_on(s, k)
+
+            @pl.when(up | down)
+            def _():
+                one = w.at[s, 0, pl.ds(0, PIECE)]
+                pltpu.make_async_copy(one, one, pass_send.at[s, k]).wait()
+
+            return carry
+
+        lax.fori_loop(0, NSTEP, drain_body, 0)
+
+    drain(0)
 
     def tile_of(n):
         u, mine = n // 2, n % 2 == 0
@@ -341,82 +387,100 @@
             send_sem=rs_send, recv_sem=relay_recv.at[n], device_id=device, device_id_type=MESH,
         )
 
-    def sum_copy(n, rel, side, device):
+    def sum_copy(n, lane, side, device):
         rows = tile_rows(n)
         return pltpu.make_async_remote_copy(
-            src_ref=w.at[0, 0, rows, pl.ds(rel * 128, 128)], dst_ref=rbuf.at[side, rows],
+            src_ref=w.at[0, 1, rows, pl.ds(lane, 128)], dst_ref=rbuf.at[side, rows],
             send_sem=rs_send, recv_sem=rs_recv.at[side, n], device_id=device, device_id_type=MESH,
         )
 
-    def out_body(n, carry):
-        @pl.when((n % 2 == 0) & (n >= 8) & (n < NT))
-        def _():
-            comm_step(37 + n // 2)
-
-        @pl.when((n % 2 == 1) & (n < NT))
-        def _():
-            u = n // 2
+    def product(n, base):
+        rows = tile_rows(n)
+        dims = (((1,), (1,)), ((), ()))
+        tokens = slice(base, base + 256)
+        part = lax.dot_general(w[2, 0, rows, :], att[0, tokens], dims, preferred_element_type=F32)
+        return part + lax.dot_general(
+            w[2, 1, rows, :], att[1, tokens], dims, preferred_element_type=F32
+        )
+
+    def first_pass(n):
+        u = n // 2
+
+        @pl.when(n % 2 == 0)
+        def _():
+            lax.fori_loop(
+                jnp.maximum(pick(u, (30, 34, 37, 39, 40, 42, 43, 44)), ATT_START + 4),
+                jnp.maximum(pick(u, (34, 37, 39, 40, 42, 43, 44, 45)), ATT_START + 4),
+                step_body, 0,
+            )
+
+        @pl.when(n % 2 == 1)
+        def _():
             by_x = c == 1
             one = jnp.where(by_x, pick(u, (0, 15, 5, 6, 2, 3, 10, 9)), pick(u, (2, 5, 7, 15, 0, 11, 1, 4)))
             two = jnp.where(by_x, pick(u, (1, 4, 7, 8, 11, 12, 13, 14)), pick(u, (3, 6, 8, 9, 10, 12, 13, 14)))
             await_partner(2, one, 1)
             await_partner(2, two, 1)
 
-        @pl.when(n < NT)
-        def _():
-            rows = tile_rows(n)
-            dims = (((1,), (1,)), ((), ()))
-            part = lax.dot_general(w[2, 0, rows, :], att[0], dims, preferred_element_type=F32)
-            part += lax.dot_general(w[2, 1, rows, :], att[1], dims, preferred_element_type=F32)
-            w[0, 0, rows, :] = part.astype(BF)
-
-            @pl.when(n % 2 == 0)
-            def _():
-                relay_copy(n, yp).start()
-                sum_copy(n, 2, 1, ym).start()
-
-            @pl.when(n % 2 == 1)
-            def _():
-                relay_copy(n, ym).start()
-                sum_copy(n, 1, 0, yp).start()
-
-        @pl.when(n >= LAG)
-        def _():
-            m = n - LAG
-            rows = tile_rows(m)
-            relay_copy(m, yp).wait_recv()
-
-            @pl.when(m % 2 == 0)
-            def _():
-                merged = w[0, 0, rows, pl.ds(128, 128)].astype(F32) + relay[rows].astype(F32)
-                w[0, 0, rows, pl.ds(128, 128)] = merged.astype(BF)
-                sum_copy(m, 1, 0, yp).start()
-
-            @pl.when(m % 2 == 1)
-            def _():
-                merged = w[0, 0, rows, pl.ds(256, 128)].astype(F32) + relay[rows].astype(F32)
-                w[0, 0, rows, pl.ds(256, 128)] = merged.astype(BF)
-                sum_copy(m, 2, 1, ym).start()
-
-        return carry
-
-    lax.fori_loop(0, NT + LAG, out_body, 0)
-
-    def sum_body(n, total):
+        w[0, 0, tile_rows(n), pl.ds(0, 256)] = product(n, 0).astype(BF)
+
+        @pl.when(n % 2 == 0)
+        def _():
+            relay_copy(n, yp).start()
+
+        @pl.when(n % 2 == 1)
+        def _():
+            relay_copy(n, ym).start()
+
+        @pl.when((n < 8) & (n % 2 == 1))
+        def _():
+            attend_step(4 + n // 2)
+
+    def second_pass(n):
         rows = tile_rows(n)
-        sum_copy(n, 1, 0, yp).wait_recv()
-        sum_copy(n, 2, 1, ym).wait_recv()
+        relay_copy(n, yp).wait_recv()
+        part = product(n, 256)
+        term = relay[rows].astype(F32)
+        even = n % 2 == 0
+        w[0, 1, rows, pl.ds(0, 128)] = (part[:, :128] + jnp.where(even, term, 0.0)).astype(BF)
+        w[0, 1, rows, pl.ds(128, 128)] = (part[:, 128:] + jnp.where(even, 0.0, term)).astype(BF)
+        sum_copy(n, 0, 0, yp).start()
+        sum_copy(n, 128, 1, ym).start()
+
+    def take_sum(m):
+        rows = tile_rows(m)
+        sum_copy(m, 0, 0, yp).wait_recv()
+        sum_copy(m, 128, 1, ym).wait_recv()
         value = (
-            w[0, 0, rows, pl.ds(384, 128)].astype(F32)
+            w[0, 0, rows, pl.ds(128, 128)].astype(F32)
             + rbuf[0, rows].astype(F32)
             + rbuf[1, rows].astype(F32)
         )
         padded = jnp.concatenate([value, jnp.zeros((48, 128), F32)], axis=0)
-        proj[tile_of(n)] = padded.T
-        return total + jnp.sum(value * value, axis=0, keepdims=True)
-
-    total = lax.fori_loop(0, NT, sum_body, jnp.zeros((1, 128), F32))
-    scale = lax.rsqrt(total * (1.0 / D) + EPS)
+        proj[tile_of(m)] = padded.T
+        squares[...] += jnp.sum(value * value, axis=0, keepdims=True)
+
+    def out_body(i, carry):
+        group, at = i // (2 * GROUP), i % (2 * GROUP)
+        n = group * GROUP + at % GROUP
+
+        @pl.when((i < 2 * NT) & (at < GROUP))
+        def _():
+            first_pass(n)
+
+        @pl.when((i < 2 * NT) & (at >= GROUP))
+        def _():
+            second_pass(n)
+
+        @pl.when(i >= SUM_AT)
+        def _():
+            take_sum(i - SUM_AT)
+
+        return carry
+
+    squares[...] = jnp.zeros((1, 128), F32)
+    lax.fori_loop(0, SUM_AT + NT, out_body, 0)
+    scale = lax.rsqrt(squares[...] * (1.0 / D) + EPS)
     scale = jnp.broadcast_to(scale, (128, 128)).T[:, 0:1]
     for t in range(NT):
         cols = slice(t * PIECE, (t + 1) * PIECE)
@@ -424,10 +488,8 @@
             hid_ref[:, cols].astype(F32) + proj[t][:, :PIECE] * scale * pg_ref[:, cols]
         ).astype(BF)
 
-    for s in (1, 2):
-        sent = w.at[s, 0, pl.ds(0, NSTEP * PIECE)]
-        pltpu.make_async_copy(sent, sent, ici_send.at[s]).wait()
-        pltpu.make_async_copy(w.at[s, 0], w.at[s, 0], part_send.at[s]).wait()
+    drain(1)
+    drain(2)
     halo = kv.at[:, :, pl.ds(0, 2 * TOK)]
     pltpu.make_async_copy(halo, halo, halo_send).wait()
     summed = act.at[pl.ds(0, 3)]
@@ -464,7 +526,8 @@
             pltpu.VMEM((D, 128), BF),
             pltpu.VMEM((2, D, 128), BF),
             pltpu.VMEM((NT, 128, 384), F32),
-            dma((4,)), dma((3, NSTEP)), dma((3, NSTEP + 1)), dma((3,)), dma((3,)),
+            pltpu.VMEM((1, 128), F32),
+            dma((4,)), dma((3, NSTEP)), dma((3, NSTEP + 1)), dma((3,)), dma((3, NSTEP)), dma((3,)),
             dma((6,)), dma, dma((2, 2)), dma, dma((NT,)), dma((2, NT)), dma,
         ],
         compiler_params=pltpu.CompilerParams(

time: 196 us -> 186 us (0.949); the launches traced: 193 us -> 186 us
  Pallas kernels: 186 us -> 179 us
    pallas_call x1, Pallas kernels: 186 us -> 179 us  [per_device(): pl.pallas_call(kernel, out_shape=jax.ShapeDtypeStruct((128, D), BF), in_s...]
where the time goes in v3:
time: 186 us
  Pallas kernels  179 us (96%)
  local copies, waits for them, and re-layouts  5.21 us (3%)
  other arithmetic  2 us (1%)
    pallas_call x1, Pallas kernels, per_device(): pl.pallas_call(kernel, out_shape=jax.ShapeDtypeStruct((128, D), BF), in_s...  179 us

profile of v3, /device:TPU:0, one launch (start us, length us, event | category | flops | bytes accessed | tf_op | source)
XLA Modules:
  0.0 185.8 jit_solution(2271973618987371028)
XLA Ops:
  0.0 1.4 reshape.23.ing_ref
  1.4 1.3 reshape.26.pg_ref
  2.7 1.0 fusion
  3.7 1.0 pad_maximum_fusion
  4.7 178.5 %shard_map.91 = bf16[128,5376]{1,0:T(8,128)(2,1)} custom-call(bf16[128,5376]{1,0:T(8,128)(2,1)} %hid_ref.1, f32[1,5376]{1,0:T(1,128)} %reshape.23.ing_ref, bf16[336,512]{1,0:T(8,128)(2,1)} %wq_ref.1, bf16[336,256]{1,0:T(8,128)(2,1)} %wk_ref.1, bf16[336,256]{1,0:T(8,128)(2,1)} %wv_ref.1, bf16[336,512]{1,0:T(8,128)(2,1)} %bitcast.3, ...), custom_call_target="tpu_custom_call" | custom-call | tf_op jit(solution)/shard_map/pallas_call | solution.py:513
  183.3 2.5 %copy.11 = bf16[128,5376]{1,0:T(8,128)(2,1)} copy(bf16[128,5376]{1,0:T(8,128)(2,1)} %shard_map.91) | data formatting | bytes 2752512
  (2 shorter events, 0.0 us)

commit v4 on v3

--- a/solution.py
+++ b/solution.py
@@ -17,7 +17,7 @@
 KCH = 768
 NK = D // KCH
 NT = 16
-SUM_AT = 20
+SUM_AT = 22
 MESH = pl.DeviceIdType.MESH
 BF = jnp.bfloat16
 F32 = jnp.float32
@@ -31,7 +31,8 @@
 HALO_AT = 27
 Q_STEPS = (0, 0, 0, 0, 0, 0, 0, 30, 0, 31, 0, 32, 0, 33)
 ATT_START = 34
-GROUP = 8
+ATT_EACH = 1
+OUT_STEPS = (0, 0, 38, 0, 0, 39, 0, 0, 0, 40, 0, 0, 0, 41, 0, 0, 0, 42, 0, 0, 43, 0, 0, 0, 44, 0)
 Q_ORDER = (0, 2, 6, 1, 4, 3, 5, 2, 0, 4, 1, 3, 6, 5, 4, 2, 6, 3, 5, 0, 1, 6, 4, 0, 5, 2, 1, 3)
 Q_OTHER = (0, 6, 1, 2, 3, 4, 5, 2, 0, 1, 3, 4, 5, 6, 4, 2, 3, 0, 1, 5, 6, 6, 4, 5, 0, 1, 2, 3)
 LOG2E = 1.4426950408889634
@@ -176,7 +177,7 @@
 
     hid = hid_ref[...].astype(F32)
     mean = jnp.mean(hid * hid, axis=-1, keepdims=True)
-    act[y] = (hid * lax.rsqrt(mean + EPS) * ing_ref[...]).astype(BF)
+    act[y] = (hid * lax.rsqrt(mean + EPS) * ing_ref[...].reshape(1, D)).astype(BF)
     loads[2].wait()
     loads[3].wait()
 
@@ -346,7 +347,7 @@
 
     def attend_body(it, carry):
         attend_step(it)
-        comm_step(ATT_START + it)
+        lax.fori_loop(ATT_START + ATT_EACH * it, ATT_START + ATT_EACH * (it + 1), step_body, 0)
         return carry
 
     lax.fori_loop(0, 4, attend_body, 0)
@@ -405,14 +406,6 @@
 
     def first_pass(n):
         u = n // 2
-
-        @pl.when(n % 2 == 0)
-        def _():
-            lax.fori_loop(
-                jnp.maximum(pick(u, (30, 34, 37, 39, 40, 42, 43, 44)), ATT_START + 4),
-                jnp.maximum(pick(u, (34, 37, 39, 40, 42, 43, 44, 45)), ATT_START + 4),
-                step_body, 0,
-            )
 
         @pl.when(n % 2 == 1)
         def _():
@@ -461,14 +454,22 @@
         squares[...] += jnp.sum(value * value, axis=0, keepdims=True)
 
     def out_body(i, carry):
-        group, at = i // (2 * GROUP), i % (2 * GROUP)
-        n = group * GROUP + at % GROUP
-
-        @pl.when((i < 2 * NT) & (at < GROUP))
+        pair = (i - NT) // 2
+        early = i < NT
+        first = (early & (i < 8)) | among(pair, (0, 1, 3, 5))
+        late = 2 * pick(pair, (4, 5, 4, 6, 5, 7, 6, 7)) + i % 2
+        n = jnp.where(early, i % 8, late)
+        step = pick(i, OUT_STEPS)
+
+        @pl.when(step > 0)
+        def _():
+            comm_step(step)
+
+        @pl.when((i < 2 * NT) & first)
         def _():
             first_pass(n)
 
-        @pl.when((i < 2 * NT) & (at >= GROUP))
+        @pl.when((i < 2 * NT) & jnp.logical_not(first))
         def _():
             second_pass(n)
 
@@ -482,10 +483,11 @@
     lax.fori_loop(0, SUM_AT + NT, out_body, 0)
     scale = lax.rsqrt(squares[...] * (1.0 / D) + EPS)
     scale = jnp.broadcast_to(scale, (128, 128)).T[:, 0:1]
+    post = pg_ref[...].reshape(1, D)
     for t in range(NT):
         cols = slice(t * PIECE, (t + 1) * PIECE)
         out_ref[:, cols] = (
-            hid_ref[:, cols].astype(F32) + proj[t][:, :PIECE] * scale * pg_ref[:, cols]
+            hid_ref[:, cols].astype(F32) + proj[t][:, :PIECE] * scale * post[:, cols]
         ).astype(BF)
 
     drain(1)
@@ -535,7 +537,7 @@
         ),
     )(
         hidden_in,
-        in_gain.reshape(1, D),
+        in_gain,
         query_weight,
         key_weight,
         value_weight,
@@ -544,7 +546,7 @@
         sin_table,
         q_gain.reshape(1, HEAD),
         k_gain.reshape(1, HEAD),
-        post_gain.reshape(1, D),
+        post_gain,
     )
 
 

time: 186 us -> 184 us (0.989)
  local copies, waits for them, and re-layouts: 5.21 us -> 2.51 us
    reshape x2 -> x0, local copies, waits for them, and re-layouts: 2.71 us -> none  [the longest x1 1.36 us: per_device(): in_gain.reshape(1, D)]
where the time goes in v4:
time: 184 us; the launch traced here: 183 us
  Pallas kernels  179 us (97%)
  local copies, waits for them, and re-layouts  2.51 us (1%)
  other arithmetic  2.01 us (1%)
    pallas_call x1, Pallas kernels, per_device(): pl.pallas_call(kernel, out_shape=jax.ShapeDtypeStruct((128, D), BF), in_s...  179 us

profile of v4, /device:TPU:0, one launch (start us, length us, event | category | flops | bytes accessed | tf_op | source)
XLA Modules:
  0.0 183.3 jit_solution(16881669452284308260)
XLA Ops:
  0.0 1.0 fusion
  1.0 1.0 pad_maximum_fusion
  2.0 178.8 %shard_map.91 = bf16[128,5376]{1,0:T(8,128)(2,1)} custom-call(bf16[128,5376]{1,0:T(8,128)(2,1)} %hid_ref.1, f32[5376]{0:T(1024)} %ing_ref.1, bf16[336,512]{1,0:T(8,128)(2,1)} %wq_ref.1, bf16[336,256]{1,0:T(8,128)(2,1)} %wk_ref.1, bf16[336,256]{1,0:T(8,128)(2,1)} %wv_ref.1, bf16[336,512]{1,0:T(8,128)(2,1)} %bitcast.3, f32[512,128]{1,0:T(8,128)} %get-tuple-element.8.cos_ref, ...), custom_call_target="tpu_custom_call" | custom-call | tf_op jit(solution)/shard_map/pallas_call | solution.py:515
  180.8 2.5 %copy.11 = bf16[128,5376]{1,0:T(8,128)(2,1)} copy(bf16[128,5376]{1,0:T(8,128)(2,1)} %shard_map.91) | data formatting | bytes 2752512
  (2 shorter events, 0.0 us)

commit v5 on v4

--- a/solution.py
+++ b/solution.py
@@ -332,8 +332,10 @@
         )
         scores = scores.reshape(2, 128, 1152) * (SCALE * LOG2E) + bias[qc][None]
         expo = jnp.exp2(scores - jnp.max(scores, axis=-1, keepdims=True))
-        weights = (expo * (1.0 / jnp.sum(expo, axis=-1, keepdims=True))).astype(BF)
-        mixed = jnp.dot(weights.reshape(256, 1152), values, preferred_element_type=F32).astype(BF)
+        total = jnp.sum(expo, axis=-1, keepdims=True).reshape(256, 1)
+        weights = expo.astype(BF).reshape(256, 1152)
+        mixed = jnp.dot(weights, values, preferred_element_type=F32)
+        mixed = (mixed * (1.0 / total)).astype(BF)
         rows = pl.ds(pl.multiple_of(rel * 128, 128), 128)
         for h in range(2):
             lanes = pl.ds(pl.multiple_of((kvh % 2) * 256 + h * 128, 128), 128)
@@ -449,8 +451,8 @@
             + rbuf[0, rows].astype(F32)
             + rbuf[1, rows].astype(F32)
         )
-        padded = jnp.concatenate([value, jnp.zeros((48, 128), F32)], axis=0)
-        proj[tile_of(m)] = padded.T
+        padded = jnp.concatenate([value, jnp.zeros((176, 128), F32)], axis=0)
+        proj[tile_of(m)] = pltpu.roll(padded.T, (tile_of(m) * PIECE) % 128, 1)
         squares[...] += jnp.sum(value * value, axis=0, keepdims=True)
 
     def out_body(i, carry):
@@ -484,10 +486,14 @@
     scale = lax.rsqrt(squares[...] * (1.0 / D) + EPS)
     scale = jnp.broadcast_to(scale, (128, 128)).T[:, 0:1]
     post = pg_ref[...].reshape(1, D)
-    for t in range(NT):
-        cols = slice(t * PIECE, (t + 1) * PIECE)
+    for lane in range(0, D, 128):
+        value = 0.0
+        for t in range(lane // PIECE, (lane + 127) // PIECE + 1):
+            at = lane - t * PIECE // 128 * 128
+            value += proj[t, :, at : at + 128]
+        cols = slice(lane, lane + 128)
         out_ref[:, cols] = (
-            hid_ref[:, cols].astype(F32) + proj[t][:, :PIECE] * scale * post[:, cols]
+            hid_ref[:, cols].astype(F32) + value * scale * post[:, cols]
         ).astype(BF)
 
     drain(1)
@@ -527,7 +533,7 @@
             pltpu.VMEM((4, 128, 1152), F32),
             pltpu.VMEM((D, 128), BF),
             pltpu.VMEM((2, D, 128), BF),
-            pltpu.VMEM((NT, 128, 384), F32),
+            pltpu.VMEM((NT, 128, 512), F32),
             pltpu.VMEM((1, 128), F32),
             dma((4,)), dma((3, NSTEP)), dma((3, NSTEP + 1)), dma((3,)), dma((3, NSTEP)), dma((3,)),
             dma((6,)), dma, dma((2, 2)), dma, dma((NT,)), dma((2, NT)), dma,

time: 184 us -> 180 us (0.978)
  Pallas kernels: 179 us -> 176 us
    pallas_call x1, Pallas kernels: 179 us -> 176 us  [per_device(): pl.pallas_call(kernel, out_shape=jax.ShapeDtypeStruct((128, D), BF), in_s...]
where the time goes in v5:
time: 180 us
  Pallas kernels  176 us (98%)
  local copies, waits for them, and re-layouts  2.51 us (1%)
  other arithmetic  2.01 us (1%)
    pallas_call x1, Pallas kernels, per_device(): pl.pallas_call(kernel, out_shape=jax.ShapeDtypeStruct((128, D), BF), in_s...  176 us

profile of v5, /device:TPU:0, one launch (start us, length us, event | category | flops | bytes accessed | tf_op | source)
XLA Modules:
  0.0 180.2 jit_solution(14764056178740589668)
XLA Ops:
  0.0 1.0 fusion
  1.0 1.0 pad_maximum_fusion
  2.0 175.7 %shard_map.91 = bf16[128,5376]{1,0:T(8,128)(2,1)} custom-call(bf16[128,5376]{1,0:T(8,128)(2,1)} %hid_ref.1, f32[5376]{0:T(1024)} %ing_ref.1, bf16[336,512]{1,0:T(8,128)(2,1)} %wq_ref.1, bf16[336,256]{1,0:T(8,128)(2,1)} %wk_ref.1, bf16[336,256]{1,0:T(8,128)(2,1)} %wv_ref.1, bf16[336,512]{1,0:T(8,128)(2,1)} %bitcast.3, f32[512,128]{1,0:T(8,128)} %get-tuple-element.8.cos_ref, ...), custom_call_target="tpu_custom_call" | custom-call | tf_op jit(solution)/shard_map/pallas_call | solution.py:521
  177.7 2.5 %copy.11 = bf16[128,5376]{1,0:T(8,128)(2,1)} copy(bf16[128,5376]{1,0:T(8,128)(2,1)} %shard_map.91) | data formatting | bytes 2752512
  (2 shorter events, 0.0 us)

commit v6 on v5

--- a/solution.py
+++ b/solution.py
@@ -17,7 +17,7 @@
 KCH = 768
 NK = D // KCH
 NT = 16
-SUM_AT = 22
+SUM_AT = 20
 MESH = pl.DeviceIdType.MESH
 BF = jnp.bfloat16
 F32 = jnp.float32
@@ -278,9 +278,20 @@
 
         @pl.when(g == HALO_AT)
         def _():
+            near = (c == 1) & (xh == 0)
+
+            @pl.when(near)
+            def _():
+                for half in range(2):
+                    halo_copy(half, 2).start()
+
             for half in range(2):
                 halo_copy(half, 1).start()
-                halo_copy(half, 2).start()
+
+            @pl.when(jnp.logical_not(near))
+            def _():
+                for half in range(2):
+                    halo_copy(half, 2).start()
 
         return carry
 
@@ -511,11 +522,11 @@
     ctx, tp = lax.axis_index("ctx"), lax.axis_index("tp")
     block = ctx * 2 + tp // 4
     positions = block * TOK + jnp.arange(TOK, dtype=jnp.int32)
-    frequency = 10000.0 ** (-(jnp.arange(HEAD // 2, dtype=F32) * 2.0 / HEAD))
+    lane = jnp.arange(HEAD, dtype=jnp.int32)
+    frequency = 10000.0 ** (-((lane % (HEAD // 2)).astype(F32) * 2.0 / HEAD))
     angles = positions.astype(F32)[:, None] * frequency[None, :]
-    cosine, sine = jnp.cos(angles), jnp.sin(angles)
-    cos_table = jnp.concatenate([cosine, cosine], axis=-1)
-    sin_table = jnp.concatenate([-sine, sine], axis=-1)
+    cos_table = jnp.cos(angles)
+    sin_table = jnp.sin(angles) * jnp.where(lane < HEAD // 2, -1.0, 1.0)[None, :]
     vmem, hbm = pl.BlockSpec(memory_space=pltpu.VMEM), pl.BlockSpec(memory_space=pl.ANY)
     dma = pltpu.SemaphoreType.DMA
     return pl.pallas_call(

time: 180 us -> 180 us (level); the launches traced: 180 us -> 178 us
  Pallas kernels: 176 us -> 174 us
    pallas_call x1, Pallas kernels: 176 us -> 174 us  [per_device(): pl.pallas_call(kernel, out_shape=jax.ShapeDtypeStruct((128, D), BF), in_s...]
    mul x0 -> x1, other arithmetic: none -> 1.83 us  [per_device(): jnp.sin(angles) * jnp.where(lane < HEAD // 2, -1.0, 1.0)[None, :]]
where the time goes in v6:
time: 180 us; the launch traced here: 178 us
  Pallas kernels  174 us (97%)
  local copies, waits for them, and re-layouts  2.51 us (1%)
  other arithmetic  1.84 us (1%)
    pallas_call x1, Pallas kernels, per_device(): pl.pallas_call(kernel, out_shape=jax.ShapeDtypeStruct((128, D), BF), in_s...  174 us

profile of v6, /device:TPU:0, one launch (start us, length us, event | category | flops | bytes accessed | tf_op | source)
XLA Modules:
  0.0 178.1 jit_solution(13941436504532038895)
XLA Ops:
  0.0 1.8 %fusion = (f32[512,128]{1,0:T(8,128)}, f32[512,128]{1,0:T(8,128)}) fusion(f32[128]{0:T(128)S(1)} %get-tuple-element.7, f32[128]{0:T(128)S(1)} %get-tuple-element.8, f32[512]{0:T(512)S(1)} %add_convert_fusion), kind=kLoop, calls=%fused_computation.2 | loop fusion | flops 131072 | bytes 527360 | tf_op jit(solution)/shard_map/mul | solution.py:529
  1.8 173.8 %shard_map.91 = bf16[128,5376]{1,0:T(8,128)(2,1)} custom-call(bf16[128,5376]{1,0:T(8,128)(2,1)} %hid_ref.1, f32[5376]{0:T(1024)} %ing_ref.1, bf16[336,512]{1,0:T(8,128)(2,1)} %wq_ref.1, bf16[336,256]{1,0:T(8,128)(2,1)} %wk_ref.1, bf16[336,256]{1,0:T(8,128)(2,1)} %wv_ref.1, bf16[336,512]{1,0:T(8,128)(2,1)} %bitcast.3, f32[512,128]{1,0:T(8,128)} %get-tuple-element.6.cos_ref, ...), custom_call_target="tpu_custom_call" | custom-call | tf_op jit(solution)/shard_map/pallas_call | solution.py:532
  175.6 2.5 %copy.11 = bf16[128,5376]{1,0:T(8,128)(2,1)} copy(bf16[128,5376]{1,0:T(8,128)(2,1)} %shard_map.91) | data formatting | bytes 2752512
  (2 shorter events, 0.0 us)
